TPU v7x, 32 devices: a whole 2x2x4 slice. The times are simulated.
32 devices in a mesh: blk: 8 (over y, x, core), rows: 4 (over z).
Axes of the slice: x: 2, y: 2, z: 4, core: 2. Of those that a mesh axis runs over, the one named last changes fastest.
Arguments:
- cholesky: bfloat16 [4096, 256, 256], P('blk', 'rows'), may hold values from -0.01171875 to 0.01171875
- green: bfloat16 [256, 256, 256], P('blk', 'rows'), may hold values from -18 to 18
- aux_field: float32 [256, 4096], P(None, 'blk'), may hold values from -6 to 6
- walker_orbitals: bfloat16 [256, 256, 128], P('blk', 'rows'), may hold values from -6 to 6
Outputs:
- new_orbitals: float32 [256, 256, 128], P('blk', 'rows')
- force_bias: float32 [256, 4096], P(None, 'blk')
All inputs are finite; a program needn't handle non-finite values.
Results may differ from a plain program's by a relative error of at most 0.025.
Values may be sent and summed in bfloat16 or wider, within the bound.
No kernel may reach another device: no remote copies, remote signals or barrier semaphores. Data moves between devices by JAX's collectives and lax.ppermute only.
A program may use at most 128 MiB of HBM per device.

v0:
```python
import functools

import jax
import jax.numpy as jnp
from jax import lax
from jax.experimental import pallas as pl
from jax.experimental.pallas import tpu as pltpu
from jax.sharding import PartitionSpec as P


TAYLOR = 4
CHUNKS = 2
PARTS = 2

time_root = 0.5
F32, BF16 = jnp.float32, jnp.bfloat16


def spread(core, rel, bits):
    if core == 0:
        return rel
    return sum(((rel >> t) & 1) << (bits - 1 - t) for t in range(bits))


def vmem_limit():
    return pltpu.CompilerParams(vmem_limit_bytes=56 << 20)


def relayout_kernel(which, block, out):
    out[...] = jnp.swapaxes(block[...], 0, 1)


def vectors_inner(cholesky, which, part):
    vecs, rows, orbitals = cholesky.shape
    half = rows // 2 // PARTS
    depth, width = min(16, half), min(256, vecs)
    which = (which * PARTS + part).astype(jnp.int32)
    return pl.pallas_call(
        relayout_kernel,
        out_shape=jax.ShapeDtypeStruct((half, vecs, orbitals), BF16),
        grid_spec=pltpu.PrefetchScalarGridSpec(
            num_scalar_prefetch=1,
            grid=(half // depth, vecs // width),
            in_specs=[
                pl.BlockSpec(
                    (width, depth, orbitals), lambda i, g, c: (g, c[0] * (half // depth) + i, 0)
                )
            ],
            out_specs=pl.BlockSpec((depth, width, orbitals), lambda i, g, c: (i, g, 0)),
        ),
        cost_estimate=pl.CostEstimate(
            flops=0, bytes_accessed=4 * half * vecs * orbitals, transcendentals=0
        ),
        compiler_params=vmem_limit(),
        name="relayout",
    )(which.reshape(1), cholesky)


def bias_kernel(order, *refs, pieces, steps, last):
    greens, (kept, swapped), rest = refs[:pieces], refs[pieces : pieces + 2], refs[pieces + 2 :]
    before, rest = (rest[:2], rest[2:]) if last else ((), rest)
    outs, accs = (rest[:2], rest[2:]) if last else (rest, rest)
    step = pl.program_id(0)
    depth = kept.shape[0]
    fields = jnp.concatenate(
        [jnp.concatenate([g[i] for g in greens], axis=0) for i in range(depth)], axis=1
    )
    for side, (chol, acc) in enumerate(zip((kept, swapped), accs)):
        vectors = jnp.concatenate([chol[i] for i in range(depth)], axis=1)
        part = lax.dot_general(
            fields, vectors, (((1,), (1,)), ((), ())), preferred_element_type=F32
        )

        @pl.when(step == 0)
        def _():
            acc[...] = part + before[side][...] if last else part

        @pl.when(step > 0)
        def _():
            acc[...] += part

    if last:

        @pl.when(step == steps - 1)
        def _():
            for acc, out in zip(accs, outs):
                rows = out.shape[1] // (2 * pieces)
                for b in range(2 * pieces):
                    to = pl.ds(pl.multiple_of(order[b] * rows, rows), rows)
                    for c in range(CHUNKS):
                        first = (b * CHUNKS + c) * rows
                        out[c, to, :] = acc[first : first + rows, :].astype(out.dtype)


def bias_parts(order, greens, kept, swapped, part, before):
    rows_part, vecs, orbitals = kept.shape
    pieces = len(greens)
    walkers = pieces * greens[0].shape[1]
    last = part == PARTS - 1
    depth = min(8, rows_part)
    steps = rows_part // depth
    flat = pl.BlockSpec((walkers, vecs), lambda i, o: (0, 0))
    chol_spec = pl.BlockSpec((depth, vecs, orbitals), lambda i, o: (i, 0, 0))
    green_spec = pl.BlockSpec((depth,) + greens[0].shape[1:], lambda i, o: (i, 0, 0))
    by_chunk = (CHUNKS, walkers // CHUNKS, vecs)
    chunk_spec = pl.BlockSpec(by_chunk, lambda i, o: (0, 0, 0))
    wide = jax.ShapeDtypeStruct((walkers, vecs), F32)
    return pl.pallas_call(
        functools.partial(bias_kernel, pieces=pieces, steps=steps, last=last),
        out_shape=(
            (jax.ShapeDtypeStruct(by_chunk, F32), jax.ShapeDtypeStruct(by_chunk, BF16))
            if last
            else (wide, wide)
        ),
        grid_spec=pltpu.PrefetchScalarGridSpec(
            num_scalar_prefetch=1,
            grid=(steps,),
            in_specs=[green_spec] * pieces + [chol_spec] * 2 + [flat] * len(before),
            out_specs=(chunk_spec, chunk_spec) if last else (flat, flat),
            scratch_shapes=[pltpu.VMEM((walkers, vecs), F32)] * (2 if last else 0),
        ),
        cost_estimate=pl.CostEstimate(
            flops=4 * walkers * rows_part * vecs * orbitals,
            bytes_accessed=4 * rows_part * vecs * orbitals + 2 * walkers * rows_part * orbitals,
            transcendentals=0,
        ),
        compiler_params=vmem_limit(),
        name="bias",
    )(order, *greens, kept, swapped, *before)


def potential_kernel(order, *refs, pieces, steps):
    shift_kept, shift_swapped = refs[:2]
    kept, swapped = refs[2 : 2 + PARTS], refs[2 + PARTS : 2 + 2 * PARTS]
    outs, (field,) = refs[2 + 2 * PARTS : -1], refs[-1:]
    vecs = shift_kept.shape[1]
    blocks = 2 * pieces
    rows = field.shape[0] // blocks

    @pl.when(pl.program_id(0) == 0)
    def _():
        for b in range(blocks):
            at = pl.ds(pl.multiple_of(order[b] * rows, rows), rows)
            field[b * rows : (b + 1) * rows, :vecs] = shift_kept[at, :]
            field[b * rows : (b + 1) * rows, vecs:] = shift_swapped[at, :]

    for p in range(PARTS):

        @pl.when(pl.program_id(0) // steps == p)
        def _():
            for i in range(kept[p].shape[0]):
                vectors = jnp.concatenate([kept[p][i], swapped[p][i]], axis=0)
                part = jnp.dot(field[...], vectors, preferred_element_type=F32).astype(BF16)
                for j, out in enumerate(outs):
                    out[i] = part[2 * j * rows : 2 * (j + 1) * rows]


def potential_parts(order, shift_kept, shift_swapped, kept, swapped, pieces):
    rows_part, vecs, orbitals = kept[0].shape
    rows = PARTS * rows_part
    walkers = shift_kept.shape[0]
    depth = min(8, rows_part)
    steps = rows_part // depth
    chol_specs = [
        pl.BlockSpec(
            (depth, vecs, orbitals), lambda i, o, p=p: (jnp.clip(i - p * steps, 0, steps - 1), 0, 0)
        )
        for p in range(PARTS)
    ]
    shift_spec = pl.BlockSpec((walkers, vecs), lambda i, o: (0, 0))
    per = walkers // pieces
    return pl.pallas_call(
        functools.partial(potential_kernel, pieces=pieces, steps=steps),
        out_shape=[jax.ShapeDtypeStruct((rows, per, orbitals), BF16)] * pieces,
        grid_spec=pltpu.PrefetchScalarGridSpec(
            num_scalar_prefetch=1,
            grid=(rows // depth,),
            in_specs=[shift_spec] * 2 + chol_specs * 2,
            out_specs=[pl.BlockSpec((depth, per, orbitals), lambda i, o: (i, 0, 0))] * pieces,
            scratch_shapes=[pltpu.VMEM((walkers, 2 * vecs), BF16)],
        ),
        cost_estimate=pl.CostEstimate(
            flops=4 * walkers * rows * vecs * orbitals,
            bytes_accessed=4 * rows * vecs * orbitals + 2 * walkers * rows * orbitals,
            transcendentals=0,
        ),
        compiler_params=vmem_limit(),
        name="potential",
    )(order, shift_kept, shift_swapped, *kept, *swapped)


def taylor_kernel(order, *refs, groups):
    pots, terms = refs[:groups], refs[groups : 2 * groups]
    outs = refs[2 * groups : 3 * groups]
    full_pot, full_term, full_sum = refs[3 * groups :]
    low = pots[0].shape[2]
    high = terms[0].shape[1]
    for s, piece in enumerate(pots):
        for h in range(2):
            at = pl.ds(pl.multiple_of(order[2 * s + h] * low, low), low)
            full_pot[:, at, :] = piece[h]
    for s, piece in enumerate(terms):
        at = pl.ds(pl.multiple_of((order[2 * s] // 2) * high, high), high)
        full_term[:, at, :] = piece[...]
    count = full_pot.shape[0]
    now = [full_term[w] for w in range(count)]
    total = [None] * count
    for degree in range(1, TAYLOR + 1):
        for w in range(count):
            product = jnp.dot(full_pot[w], now[w], preferred_element_type=F32)
            now[w] = (product / degree).astype(BF16)
            wide = now[w].astype(F32)
            total[w] = wide if degree == 1 else total[w] + wide
    for w in range(count):
        full_sum[w] = total[w].astype(BF16)
    for s, out in enumerate(outs):
        at = pl.ds(pl.multiple_of((order[2 * s] // 2) * high, high), high)
        out[...] = full_sum[:, at, :]


def taylor_sums(order, pots, terms):
    groups = len(terms)
    _, count, _, orbitals = pots[0].shape
    high, occupied = terms[0].shape[1:]
    vmem = pl.BlockSpec(memory_space=pltpu.VMEM)
    return pl.pallas_call(
        functools.partial(taylor_kernel, groups=groups),
        out_shape=[jax.ShapeDtypeStruct((count, high, occupied), BF16)] * groups,
        in_specs=[pl.BlockSpec(memory_space=pltpu.SMEM)] + [vmem] * (2 * groups),
        out_specs=[vmem] * groups,
        scratch_shapes=[
            pltpu.VMEM((count, orbitals, orbitals), BF16),
            pltpu.VMEM((count, orbitals, occupied), BF16),
            pltpu.VMEM((count, orbitals, occupied), BF16),
        ],
        cost_estimate=pl.CostEstimate(
            flops=2 * TAYLOR * count * orbitals * orbitals * occupied,
            bytes_accessed=2 * count * orbitals * (orbitals + 2 * occupied),
            transcendentals=0,
        ),
        compiler_params=vmem_limit(),
        name="taylor",
    )(order, *pots, *terms)


def propagate(cholesky, green, aux_field, walker_orbitals):
    n_blk, n_rows = lax.axis_size("blk"), lax.axis_size("rows")
    me, plane = lax.axis_index("blk"), lax.axis_index("rows")
    core = me & 1
    vecs, rows_dev, orbitals = cholesky.shape
    walk_count, _, occupied = walker_orbitals.shape
    half = rows_dev // 2
    chips = n_blk // 2
    bits = chips.bit_length() - 1
    plane_bits = n_rows.bit_length() - 1
    mine = walk_count // CHUNKS
    each = mine // n_rows

    def swap_cores(x):
        return lax.ppermute(x, "blk", [(i, i ^ 1) for i in range(n_blk)])

    def swap_chips(x, t):
        pairs = [(i, i ^ (spread(i & 1, 1 << t, bits) << 1)) for i in range(n_blk)]
        return lax.ppermute(x, "blk", pairs)

    def swap_planes(x, s):
        return lax.ppermute(x, "rows", [(z, z ^ s) for z in range(n_rows)])

    tables = [
        [(spread(c, j, bits) << 1) | h for j in range(chips) for h in range(2)] for c in range(2)
    ]
    order = me ^ jnp.where(core == 0, jnp.array(tables[0], jnp.int32), jnp.array(tables[1], jnp.int32))
    plane_order = (plane * 2 + core) ^ jnp.arange(2 * n_rows, dtype=jnp.int32)

    def row_half(x, which):
        part = lax.dynamic_slice_in_dim(x, which * half, half, 1)
        return part.transpose(1, 0, 2)

    green_kept = row_half(green, core)
    green_swapped = swap_cores(row_half(green, 1 - core))
    rows_part = half // PARTS
    starts = []
    for p in range(PARTS):
        at = slice(p * rows_part, (p + 1) * rows_part)
        starts.append(jnp.concatenate([green_kept[at], green_swapped[at]], axis=1))
    cholesky, starts = lax.optimization_barrier((cholesky, starts))
    chol_swapped, chol_kept = [], []
    for p in range(PARTS):
        chol_sent = vectors_inner(cholesky, 1 - core, p)
        chol_swapped.append(swap_cores(chol_sent))
    for p in range(PARTS):
        chol_kept.append(vectors_inner(cholesky, core, p))

    own = walker_orbitals.reshape(CHUNKS, n_rows, each, rows_dev, occupied)
    terms = [
        lax.dynamic_index_in_dim(own, plane ^ s, 1, keepdims=False) for s in range(n_rows)
    ]
    terms = [swap_planes(x, s) if s else x for s, x in enumerate(terms)]

    def gather_green(p):
        gathered = [starts[p]]
        for t in range(bits):
            gathered += [swap_chips(piece, t) for piece in gathered]
        return gathered

    def full_bias(c, bias_kept, bias_swapped):
        bias = bias_kept[c] + bias_swapped[c].astype(F32)
        for t in range(plane_bits):
            bias = bias.astype(BF16)
            bias = bias.astype(F32) + swap_planes(bias, 1 << t).astype(F32)
        return bias

    def scatter_potential(c, bias):
        walkers = bias.shape[0]
        aux = aux_field.reshape(n_blk, walk_count, vecs)[:, c * mine : (c + 1) * mine]
        shifted = (time_root * (aux.reshape(walkers, vecs) - bias)).astype(BF16)
        shifted_swapped = swap_cores(shifted)
        acc = potential_parts(order, shifted, shifted_swapped, chol_kept, chol_swapped, chips)
        total = [a.astype(F32) for a in acc]
        for t in reversed(range(bits)):
            for j in reversed(range(1 << t)):
                sent = total[j + (1 << t)].astype(BF16)
                total[j] = total[j] + swap_chips(sent, t).astype(F32)
        potential = total[0].astype(BF16).transpose(1, 0, 2)
        return potential.reshape(2, n_rows, each, half, orbitals)

    def propagated(c, potential):
        swapped = swap_cores(potential[1])
        sides = jnp.stack([potential[0], swapped])
        pots = [
            lax.dynamic_index_in_dim(sides, plane ^ s, 1, keepdims=False) for s in range(n_rows)
        ]
        pots = [swap_planes(p, s) if s else p for s, p in enumerate(pots)]
        sums = taylor_sums(plane_order, pots, [t[c] for t in terms])
        result = jnp.zeros((n_rows, each, rows_dev, occupied), BF16)
        for s in range(n_rows):
            got = swap_planes(sums[s], s) if s else sums[s]
            result = lax.dynamic_update_index_in_dim(result, got, plane ^ s, 0)
        return result.reshape(mine, rows_dev, occupied)

    gathered = [gather_green(p) for p in range(PARTS)]
    parts = ()
    for p in range(PARTS):
        parts = bias_parts(order, gathered[p], chol_kept[p], chol_swapped[p], p, parts)
    bias_kept, bias_swapped = parts[0], swap_cores(parts[1])
    biases = [full_bias(c, bias_kept, bias_swapped) for c in range(CHUNKS)]
    potentials = [scatter_potential(c, biases[c]) for c in range(CHUNKS)]
    sums = jnp.concatenate([propagated(c, potentials[c]) for c in range(CHUNKS)], axis=0)
    force_bias = jnp.stack([b.reshape(n_blk, mine, vecs) for b in biases], axis=1)
    force_bias = force_bias.reshape(-1, vecs)
    return walker_orbitals.astype(F32) + sums.astype(F32), force_bias


def solution(mesh):
    return jax.shard_map(
        propagate,
        mesh=mesh,
        in_specs=(
            P("blk", "rows", None),
            P("blk", "rows", None),
            P(None, "blk"),
            P("blk", "rows", None),
        ),
        out_specs=(P("blk", "rows", None), P(None, "blk")),
        check_vma=False,
    )
```

profile of v0, /device:TPU:0, one launch (start us, length us, event | category | flops | bytes accessed | tf_op | source)
XLA Modules:
  0.0 196.8 jit_solution(12465215509881614895)
XLA Ops:
  0.6 1.3 constant_dynamic-slice_fusion.1
  3.1 1.2 collective-permute-done
  4.5 4.6 %relayout.7 = bf16[16,512,256]{2,1,0:T(8,128)(2,1)} custom-call(s32[1]{0:T(128)} %bitcast.7.which, bf16[512,64,256]{2,1,0:T(8,128)(2,1)} %block.3), custom_call_target="tpu_custom_call" | custom-call | bytes 8388608 | tf_op jit(solution)/shard_map/relayout/pallas_call | solution.py:38
  9.4 4.2 %relayout.5 = bf16[16,512,256]{2,1,0:T(8,128)(2,1)} custom-call(s32[1]{0:T(128)} %bitcast.5.which, bf16[512,64,256]{2,1,0:T(8,128)(2,1)} %block.3), custom_call_target="tpu_custom_call" | custom-call | bytes 8388608 | tf_op jit(solution)/shard_map/relayout/pallas_call | solution.py:38
  13.8 2.8 %collective-permute-start.5 = (bf16[16,64,256]{2,1,0:T(8,128)(2,1)S(1)}, bf16[16,64,256]{2,1,0:T(8,128)(2,1)S(1)}, u32[]{:S(2)}, u32[]{:S(2)}) collective-permute-start(bf16[16,64,256]{2,1,0:T(8,128)(2,1)S(1)} %get-tuple-element.27.refs_0_), channel_id=1, source_target_pairs={{0,8},{4,20},{8,0},{12,28},{16,24},{20,4},{24,16},{28,12},{1,9},{5... | collective-permute-start | bytes 1572872 | tf_op jit(solution)/shard_map/ppermute | solution.py:264
  16.6 1.5 collective-permute-start.6
  18.7 9.8 %collective-permute-done.5.refs_1_ = bf16[16,64,256]{2,1,0:T(8,128)(2,1)S(1)} collective-permute-done((bf16[16,64,256]{2,1,0:T(8,128)(2,1)S(1)}, bf16[16,64,256]{2,1,0:T(8,128)(2,1)S(1)}, u32[]{:S(2)}, u32[]{:S(2)}) %collective-permute-start.5) | collective-permute-done | bytes 524320 | tf_op jit(solution)/shard_map/ppermute | solution.py:264
  28.5 2.1 %collective-permute-start.7 = (bf16[16,64,256]{2,1,0:T(8,128)(2,1)S(1)}, bf16[16,64,256]{2,1,0:T(8,128)(2,1)}, u32[]{:S(2)}, u32[]{:S(2)}) collective-permute-start(bf16[16,64,256]{2,1,0:T(8,128)(2,1)S(1)} %collective-permute-done.5.refs_1_), channel_id=1, source_target_pairs={{0,16},{4,12},{8,24},{12,4},{16,0},{20,28},{24,8},{28,20},{1,17},{... | collective-permute-start | bytes 1572872 | tf_op jit(solution)/shard_map/ppermute | solution.py:264
  31.4 1.5 collective-permute-start.2
  32.9 6.4 %collective-permute-done.1.refs_1_ = bf16[16,64,256]{2,1,0:T(8,128)(2,1)S(1)} collective-permute-done((bf16[16,64,256]{2,1,0:T(8,128)(2,1)S(1)}, bf16[16,64,256]{2,1,0:T(8,128)(2,1)S(1)}, u32[]{:S(2)}, u32[]{:S(2)}) %collective-permute-start.1) | collective-permute-done | bytes 524320 | tf_op jit(solution)/shard_map/ppermute | solution.py:264
  39.3 1.4 collective-permute-start.3
  41.3 4.3 %relayout.6.refs_4_.refs_2_ = bf16[16,512,256]{2,1,0:T(8,128)(2,1)} custom-call(s32[1]{0:T(128)} %bitcast.6.which, bf16[512,64,256]{2,1,0:T(8,128)(2,1)} %block.3), custom_call_target="tpu_custom_call" | custom-call | bytes 8388608 | tf_op jit(solution)/shard_map/relayout/pallas_call | solution.py:38
  45.6 4.2 %relayout.4.refs_4_.refs_3_ = bf16[16,512,256]{2,1,0:T(8,128)(2,1)} custom-call(s32[1]{0:T(128)} %bitcast.4.which, bf16[512,64,256]{2,1,0:T(8,128)(2,1)} %block.3), custom_call_target="tpu_custom_call" | custom-call | bytes 8388608 | tf_op jit(solution)/shard_map/relayout/pallas_call | solution.py:38
  49.8 7.3 %bias.2 = (f32[256,512]{1,0:T(8,128)}, f32[256,512]{1,0:T(8,128)}) custom-call(s32[8]{0:T(128)} %fusion.24.order, bf16[16,64,256]{2,1,0:T(8,128)(2,1)} %copy-done.2, bf16[16,64,256]{2,1,0:T(8,128)(2,1)} %copy-done.12, bf16[16,64,256]{2,1,0:T(8,128)(2,1)} %copy-done.13, bf16[16,64,256]{2,1,0:T(8,128)(2,1)} %collective-permute-done.7.refs_3_, ...), custom_call_target="tpu_custom_call" | custom-call | flops 2147483648 | bytes 10485760 | tf_op jit(solution)/shard_map/bias/pallas_call | solution.py:108
  58.1 7.9 %bias.3 = (f32[2,128,512]{2,1,0:T(8,128)}, bf16[2,128,512]{2,1,0:T(8,128)(2,1)}) custom-call(s32[8]{0:T(128)} %fusion.24.order, bf16[16,64,256]{2,1,0:T(8,128)(2,1)} %copy-done, bf16[16,64,256]{2,1,0:T(8,128)(2,1)} %copy-done.6, bf16[16,64,256]{2,1,0:T(8,128)(2,1)} %copy-done.7, bf16[16,64,256]{2,1,0:T(8,128)(2,1)} %copy-done.8, ...), custom_call_target="tpu_custom_call" | custom-call | flops 2147483648 | bytes 10485760 | tf_op jit(solution)/shard_map/bias/pallas_call | solution.py:108
  66.0 1.7 collective-permute-done.9
  67.8 1.1 fusion.6
  68.9 2.1 %collective-permute-start.10 = (bf16[128,512]{1,0:T(8,128)(2,1)S(1)}, bf16[128,512]{1,0:T(8,128)(2,1)S(1)}, u32[]{:S(2)}, u32[]{:S(2)}) collective-permute-start(bf16[128,512]{1,0:T(8,128)(2,1)S(1)} %get-tuple-element.50), channel_id=1, source_target_pairs={{0,1},{1,0},{2,3},{3,2},{4,5},{5,4},{6,7},{7,6},{8,9},{9,8},{10,11... | collective-permute-start | bytes 393224 | tf_op jit(solution)/shard_map/ppermute | solution.py:267
  71.1 4.2 %collective-permute-done.10 = bf16[128,512]{1,0:T(8,128)(2,1)S(1)} collective-permute-done((bf16[128,512]{1,0:T(8,128)(2,1)S(1)}, bf16[128,512]{1,0:T(8,128)(2,1)S(1)}, u32[]{:S(2)}, u32[]{:S(2)}) %collective-permute-start.10) | collective-permute-done | bytes 131104 | tf_op jit(solution)/shard_map/ppermute | solution.py:267
  75.3 3.1 %collective-permute-start.11 = (bf16[128,512]{1,0:T(8,128)(2,1)S(1)}, bf16[128,512]{1,0:T(8,128)(2,1)S(1)}, u32[]{:S(2)}, u32[]{:S(2)}) collective-permute-start(bf16[128,512]{1,0:T(8,128)(2,1)S(1)} %add_convert_fusion.6), channel_id=1, source_target_pairs={{0,2},{1,3},{2,0},{3,1},{4,6},{5,7},{6,4},{7,5},{8,10},{9,11},{10,... | collective-permute-start | bytes 393224 | tf_op jit(solution)/shard_map/ppermute | solution.py:267
  78.5 2.8 %collective-permute-start.27 = (bf16[128,512]{1,0:T(8,128)(2,1)S(1)}, bf16[128,512]{1,0:T(8,128)(2,1)S(1)}, u32[]{:S(2)}, u32[]{:S(2)}) collective-permute-start(bf16[128,512]{1,0:T(8,128)(2,1)S(1)} %add_convert_fusion.4), channel_id=1, source_target_pairs={{0,2},{1,3},{2,0},{3,1},{4,6},{5,7},{6,4},{7,5},{8,10},{9,11},{10,... | collective-permute-start | bytes 393224 | tf_op jit(solution)/shard_map/ppermute | solution.py:267
  81.3 6.2 %collective-permute-done.11 = bf16[128,512]{1,0:T(8,128)(2,1)S(1)} collective-permute-done((bf16[128,512]{1,0:T(8,128)(2,1)S(1)}, bf16[128,512]{1,0:T(8,128)(2,1)S(1)}, u32[]{:S(2)}, u32[]{:S(2)}) %collective-permute-start.11) | collective-permute-done | bytes 131104 | tf_op jit(solution)/shard_map/ppermute | solution.py:267
  87.6 1.7 collective-permute-done.27
  90.1 10.3 %potential.2 = (bf16[32,32,256]{2,1,0:T(8,128)(2,1)}, bf16[32,32,256]{2,1,0:T(8,128)(2,1)}, bf16[32,32,256]{2,1,0:T(8,128)(2,1)}, bf16[32,32,256]{2,1,0:T(8,128)(2,1)}) custom-call(s32[8]{0:T(128)} %fusion.24.order, bf16[128,512]{1,0:T(8,128)(2,1)} %copy-done.4, bf16[128,512]{1,0:T(8,128)(2,1)} %copy-done.15, bf16[16,512,256]{2,1,0:T(8,128)(2,1)} %relayout.6.refs_4_.refs_2_, ...), custom_call_target="tpu_custom_call" | custom-call | flops 2147483648 | bytes 18874368 | tf_op jit(solution)/shard_map/potential/pallas_call | solution.py:172
  100.4 1.6 collective-permute-start.14
  102.1 3.3 %collective-permute-start.22 = (bf16[2,4,64,128]{3,2,1,0:T(8,128)(2,1)S(1)}, bf16[2,4,64,128]{3,2,1,0:T(8,128)(2,1)S(1)}, u32[]{:S(2)}, u32[]{:S(2)}) collective-permute-start(bf16[2,4,64,128]{3,2,1,0:T(8,128)(2,1)S(1)} %get-tuple-element.62), channel_id=1, source_target_pairs={{0,3},{1,2},{2,1},{3,0},{4,7},{5,6},{6,5},{7,4},{8,11},{9,10},{10,... | collective-permute-start | bytes 393224 | tf_op jit(solution)/shard_map/ppermute | solution.py:267
  105.4 1.1 collective-permute-start.20
  107.9 10.3 %potential.3 = (bf16[32,32,256]{2,1,0:T(8,128)(2,1)}, bf16[32,32,256]{2,1,0:T(8,128)(2,1)}, bf16[32,32,256]{2,1,0:T(8,128)(2,1)}, bf16[32,32,256]{2,1,0:T(8,128)(2,1)}) custom-call(s32[8]{0:T(128)} %fusion.24.order, bf16[128,512]{1,0:T(8,128)(2,1)} %copy-done.3, bf16[128,512]{1,0:T(8,128)(2,1)} %copy-done.14, bf16[16,512,256]{2,1,0:T(8,128)(2,1)} %relayout.6.refs_4_.refs_2_, ...), custom_call_target="tpu_custom_call" | custom-call | flops 2147483648 | bytes 18874368 | tf_op jit(solution)/shard_map/potential/pallas_call | solution.py:172
  119.2 1.6 collective-permute-start.13
  121.0 1.5 collective-permute-start.15
  123.1 9.8 %collective-permute-done.30 = bf16[32,32,256]{2,1,0:T(8,128)(2,1)S(1)} collective-permute-done((bf16[32,32,256]{2,1,0:T(8,128)(2,1)}, bf16[32,32,256]{2,1,0:T(8,128)(2,1)S(1)}, u32[]{:S(2)}, u32[]{:S(2)}) %collective-permute-start.30) | collective-permute-done | bytes 524320 | tf_op jit(solution)/shard_map/ppermute | solution.py:264
  132.9 1.2 add_convert_fusion.1
  134.1 1.8 collective-permute-start.31
  136.6 7.6 %collective-permute-done.13 = bf16[32,32,256]{2,1,0:T(8,128)(2,1)S(1)} collective-permute-done((bf16[32,32,256]{2,1,0:T(8,128)(2,1)S(1)}, bf16[32,32,256]{2,1,0:T(8,128)(2,1)S(1)}, u32[]{:S(2)}, u32[]{:S(2)}) %collective-permute-start.13) | collective-permute-done | bytes 524320 | tf_op jit(solution)/shard_map/ppermute | solution.py:264
  144.6 5.4 %collective-permute-done.29 = bf16[32,32,256]{2,1,0:T(8,128)(2,1)S(1)} collective-permute-done((bf16[32,32,256]{2,1,0:T(8,128)(2,1)}, bf16[32,32,256]{2,1,0:T(8,128)(2,1)S(1)}, u32[]{:S(2)}, u32[]{:S(2)}) %collective-permute-start.29) | collective-permute-done | bytes 524320 | tf_op jit(solution)/shard_map/ppermute | solution.py:264
  153.0 3.0 %collective-permute-start.18 = (bf16[2,4,32,256]{3,2,1,0:T(8,128)(2,1)S(1)}, bf16[2,4,32,256]{3,2,1,0:T(8,128)(2,1)S(1)}, u32[]{:S(2)}, u32[]{:S(2)}) collective-permute-start(bf16[2,4,32,256]{3,2,1,0:T(8,128)(2,1)S(1)} %get-tuple-element.57), channel_id=1, source_target_pairs={{0,2},{1,3},{2,0},{3,1},{4,6},{5,7},{6,4},{7,5},{8,10},{9,11},{10,... | collective-permute-start | bytes 393224 | tf_op jit(solution)/shard_map/ppermute | solution.py:267
  157.3 3.7 %collective-permute-start.34 = (bf16[2,4,32,256]{3,2,1,0:T(8,128)(2,1)S(1)}, bf16[2,4,32,256]{3,2,1,0:T(8,128)(2,1)S(1)}, u32[]{:S(2)}, u32[]{:S(2)}) collective-permute-start(bf16[2,4,32,256]{3,2,1,0:T(8,128)(2,1)S(1)} %get-tuple-element.68), channel_id=1, source_target_pairs={{0,2},{1,3},{2,0},{3,1},{4,6},{5,7},{6,4},{7,5},{8,10},{9,11},{10,... | collective-permute-start | bytes 393224 | tf_op jit(solution)/shard_map/ppermute | solution.py:267
  162.6 3.4 %collective-permute-done.18.refs_2_ = bf16[2,4,32,256]{3,2,1,0:T(8,128)(2,1)S(1)} collective-permute-done((bf16[2,4,32,256]{3,2,1,0:T(8,128)(2,1)S(1)}, bf16[2,4,32,256]{3,2,1,0:T(8,128)(2,1)S(1)}, u32[]{:S(2)}, u32[]{:S(2)}) %collective-permute-start.18) | collective-permute-done | bytes 131104 | tf_op jit(solution)/shard_map/ppermute | solution.py:267
  166.7 2.9 %taylor.2 = (bf16[4,64,128]{2,1,0:T(8,128)(2,1)}, bf16[4,64,128]{2,1,0:T(8,128)(2,1)}, bf16[4,64,128]{2,1,0:T(8,128)(2,1)}, bf16[4,64,128]{2,1,0:T(8,128)(2,1)}) custom-call(s32[8]{0:T(128)} %iota_xor_fusion.order, bf16[2,4,32,256]{3,2,1,0:T(8,128)(2,1)} %get-tuple-element.55.refs_0_, bf16[2,4,32,256]{3,2,1,0:T(8,128)(2,1)} %copy-done.20, ...), custom_call_target="tpu_custom_call" | custom-call | flops 268435456 | bytes 1048576 | tf_op jit(solution)/shard_map/taylor/pallas_call | solution.py:226
  169.6 8.9 %collective-permute-start.23 = (bf16[4,64,128]{2,1,0:T(8,128)(2,1)}, bf16[4,64,128]{2,1,0:T(8,128)(2,1)S(1)}, u32[]{:S(2)}, u32[]{:S(2)}) collective-permute-start(bf16[4,64,128]{2,1,0:T(8,128)(2,1)} %get-tuple-element.37), channel_id=1, source_target_pairs={{0,1},{1,0},{2,3},{3,2},{4,5},{5,4},{6,7},{7,6},{8,9},{9,8},{10,11... | collective-permute-start | bytes 196616 | tf_op jit(solution)/shard_map/ppermute | solution.py:267
  179.5 1.5 collective-permute-start.25
  181.7 2.8 %taylor.3 = (bf16[4,64,128]{2,1,0:T(8,128)(2,1)}, bf16[4,64,128]{2,1,0:T(8,128)(2,1)}, bf16[4,64,128]{2,1,0:T(8,128)(2,1)}, bf16[4,64,128]{2,1,0:T(8,128)(2,1)}) custom-call(s32[8]{0:T(128)} %iota_xor_fusion.order, bf16[2,4,32,256]{3,2,1,0:T(8,128)(2,1)} %get-tuple-element.66.refs_0_, bf16[2,4,32,256]{3,2,1,0:T(8,128)(2,1)} %copy-done.18, ...), custom_call_target="tpu_custom_call" | custom-call | flops 268435456 | bytes 1048576 | tf_op jit(solution)/shard_map/taylor/pallas_call | solution.py:226
  184.6 1.0 collective-permute-start.36
  185.6 1.9 collective-permute-start.37
  189.3 1.5 collective-permute-start.38
  191.0 2.0 %collective-permute-done.37 = bf16[4,64,128]{2,1,0:T(8,128)(2,1)S(1)} collective-permute-done((bf16[4,64,128]{2,1,0:T(8,128)(2,1)}, bf16[4,64,128]{2,1,0:T(8,128)(2,1)S(1)}, u32[]{:S(2)}, u32[]{:S(2)}) %collective-permute-start.37) | collective-permute-done | bytes 65568 | tf_op jit(solution)/shard_map/ppermute | solution.py:267
  193.0 2.7 %collective-permute-done.38 = bf16[4,64,128]{2,1,0:T(8,128)(2,1)S(1)} collective-permute-done((bf16[4,64,128]{2,1,0:T(8,128)(2,1)}, bf16[4,64,128]{2,1,0:T(8,128)(2,1)S(1)}, u32[]{:S(2)}, u32[]{:S(2)}) %collective-permute-start.38) | collective-permute-done | bytes 65568 | tf_op jit(solution)/shard_map/ppermute | solution.py:267
  195.7 1.1 convert_add_fusion
  (132 shorter events, 20.2 us)
Async XLA Ops:
  2.2 2.1 %collective-permute-start = (bf16[32,32,256]{2,1,0:T(8,128)(2,1)S(1)}, bf16[32,32,256]{2,1,0:T(8,128)(2,1)S(1)}, u32[]{:S(2)}, u32[]{:S(2)}) collective-permute-start(bf16[32,32,256]{2,1,0:T(8,128)(2,1)S(1)} %bitcast.108), channel_id=1, source_target_pairs={{0,4},{4,0},{8,12},{12,8},{16,20},{20,16},{24,28},{28,24},{1,5},{5... | collective-permute-start | bytes 1572872 | tf_op jit(solution)/shard_map/ppermute | solution.py:260
  4.5 27.0 %copy-start = (bf16[16,64,256]{2,1,0:T(8,128)(2,1)}, bf16[16,64,256]{2,1,0:T(8,128)(2,1)S(1)}, u32[]{:S(2)}) copy-start(bf16[16,64,256]{2,1,0:T(8,128)(2,1)S(1)} %get-tuple-element.25.refs_0_) | copy-start | bytes 1572868
  9.0 40.7 %collective-permute-start.8 = (bf16[16,512,256]{2,1,0:T(8,128)(2,1)}, bf16[16,512,256]{2,1,0:T(8,128)(2,1)}, u32[]{:S(2)}, u32[]{:S(2)}) collective-permute-start(bf16[16,512,256]{2,1,0:T(8,128)(2,1)} %relayout.7), channel_id=1, source_target_pairs={{0,4},{4,0},{8,12},{12,8},{16,20},{20,16},{24,28},{28,24},{1,5},{5... | collective-permute-start | bytes 12582920 | tf_op jit(solution)/shard_map/ppermute | solution.py:260
  9.4 31.4 %copy-start.16 = (s32[8]{0:T(128)S(1)}, s32[8]{0:T(128)}, u32[]{:S(2)}) copy-start(s32[8]{0:T(128)} %constant.76.clone) | copy-start | bytes 100
  13.6 43.5 %collective-permute-start.4 = (bf16[16,512,256]{2,1,0:T(8,128)(2,1)}, bf16[16,512,256]{2,1,0:T(8,128)(2,1)}, u32[]{:S(2)}, u32[]{:S(2)}) collective-permute-start(bf16[16,512,256]{2,1,0:T(8,128)(2,1)} %relayout.5), channel_id=1, source_target_pairs={{0,4},{4,0},{8,12},{12,8},{16,20},{20,16},{24,28},{28,24},{1,5},{5... | collective-permute-start | bytes 12582920 | tf_op jit(solution)/shard_map/ppermute | solution.py:260
  13.8 14.8 %collective-permute-start.5 = (bf16[16,64,256]{2,1,0:T(8,128)(2,1)S(1)}, bf16[16,64,256]{2,1,0:T(8,128)(2,1)S(1)}, u32[]{:S(2)}, u32[]{:S(2)}) collective-permute-start(bf16[16,64,256]{2,1,0:T(8,128)(2,1)S(1)} %get-tuple-element.27.refs_0_), channel_id=1, source_target_pairs={{0,8},{4,20},{8,0},{12,28},{16,24},{20,4},{24,16},{28,12},{1,9},{5... | collective-permute-start | bytes 1572872 | tf_op jit(solution)/shard_map/ppermute | solution.py:264
  16.6 14.8 %collective-permute-start.6 = (bf16[16,64,256]{2,1,0:T(8,128)(2,1)S(1)}, bf16[16,64,256]{2,1,0:T(8,128)(2,1)S(1)}, u32[]{:S(2)}, u32[]{:S(2)}) collective-permute-start(bf16[16,64,256]{2,1,0:T(8,128)(2,1)S(1)} %get-tuple-element.27.refs_0_), channel_id=1, source_target_pairs={{0,16},{4,12},{8,24},{12,4},{16,0},{20,28},{24,8},{28,20},{1,17},{... | collective-permute-start | bytes 1572872 | tf_op jit(solution)/shard_map/ppermute | solution.py:264
  18.1 21.2 %collective-permute-start.1 = (bf16[16,64,256]{2,1,0:T(8,128)(2,1)S(1)}, bf16[16,64,256]{2,1,0:T(8,128)(2,1)S(1)}, u32[]{:S(2)}, u32[]{:S(2)}) collective-permute-start(bf16[16,64,256]{2,1,0:T(8,128)(2,1)S(1)} %get-tuple-element.25.refs_0_), channel_id=1, source_target_pairs={{0,8},{4,20},{8,0},{12,28},{16,24},{20,4},{24,16},{28,12},{1,9},{5... | collective-permute-start | bytes 1572872 | tf_op jit(solution)/shard_map/ppermute | solution.py:264
  28.5 17.0 %copy-start.12 = (bf16[16,64,256]{2,1,0:T(8,128)(2,1)}, bf16[16,64,256]{2,1,0:T(8,128)(2,1)S(1)}, u32[]{:S(2)}) copy-start(bf16[16,64,256]{2,1,0:T(8,128)(2,1)S(1)} %collective-permute-done.5.refs_1_) | copy-start | bytes 1572868
  28.5 21.3 %collective-permute-start.7 = (bf16[16,64,256]{2,1,0:T(8,128)(2,1)S(1)}, bf16[16,64,256]{2,1,0:T(8,128)(2,1)}, u32[]{:S(2)}, u32[]{:S(2)}) collective-permute-start(bf16[16,64,256]{2,1,0:T(8,128)(2,1)S(1)} %collective-permute-done.5.refs_1_), channel_id=1, source_target_pairs={{0,16},{4,12},{8,24},{12,4},{16,0},{20,28},{24,8},{28,20},{1,17},{... | collective-permute-start | bytes 1572872 | tf_op jit(solution)/shard_map/ppermute | solution.py:264
  31.4 14.1 %copy-start.13 = (bf16[16,64,256]{2,1,0:T(8,128)(2,1)}, bf16[16,64,256]{2,1,0:T(8,128)(2,1)S(1)}, u32[]{:S(2)}) copy-start(bf16[16,64,256]{2,1,0:T(8,128)(2,1)S(1)} %collective-permute-done.6.refs_2_) | copy-start | bytes 1572868
  31.4 25.7 %collective-permute-start.2 = (bf16[16,64,256]{2,1,0:T(8,128)(2,1)S(1)}, bf16[16,64,256]{2,1,0:T(8,128)(2,1)S(1)}, u32[]{:S(2)}, u32[]{:S(2)}) collective-permute-start(bf16[16,64,256]{2,1,0:T(8,128)(2,1)S(1)} %get-tuple-element.25.refs_0_), channel_id=1, source_target_pairs={{0,16},{4,12},{8,24},{12,4},{16,0},{20,28},{24,8},{28,20},{1,17},{... | collective-permute-start | bytes 1572872 | tf_op jit(solution)/shard_map/ppermute | solution.py:264
  39.3 17.8 %collective-permute-start.3 = (bf16[16,64,256]{2,1,0:T(8,128)(2,1)S(1)}, bf16[16,64,256]{2,1,0:T(8,128)(2,1)S(1)}, u32[]{:S(2)}, u32[]{:S(2)}) collective-permute-start(bf16[16,64,256]{2,1,0:T(8,128)(2,1)S(1)} %collective-permute-done.1.refs_1_), channel_id=1, source_target_pairs={{0,16},{4,12},{8,24},{12,4},{16,0},{20,28},{24,8},{28,20},{1,17},{... | collective-permute-start | bytes 1572872 | tf_op jit(solution)/shard_map/ppermute | solution.py:264
  58.1 12.9 %copy-start.9 = (f32[256,512]{1,0:T(8,128)S(1)}, f32[256,512]{1,0:T(8,128)}, u32[]{:S(2)}) copy-start(f32[256,512]{1,0:T(8,128)} %param.8) | copy-start | bytes 1572868
  66.0 1.7 collective-permute-start.9
  68.9 6.4 %collective-permute-start.10 = (bf16[128,512]{1,0:T(8,128)(2,1)S(1)}, bf16[128,512]{1,0:T(8,128)(2,1)S(1)}, u32[]{:S(2)}, u32[]{:S(2)}) collective-permute-start(bf16[128,512]{1,0:T(8,128)(2,1)S(1)} %get-tuple-element.50), channel_id=1, source_target_pairs={{0,1},{1,0},{2,3},{3,2},{4,5},{5,4},{6,7},{7,6},{8,9},{9,8},{10,11... | collective-permute-start | bytes 393224 | tf_op jit(solution)/shard_map/ppermute | solution.py:267
  71.0 7.4 %collective-permute-start.26 = (bf16[128,512]{1,0:T(8,128)(2,1)S(1)}, bf16[128,512]{1,0:T(8,128)(2,1)S(1)}, u32[]{:S(2)}, u32[]{:S(2)}) collective-permute-start(bf16[128,512]{1,0:T(8,128)(2,1)S(1)} %get-tuple-element.51), channel_id=1, source_target_pairs={{0,1},{1,0},{2,3},{3,2},{4,5},{5,4},{6,7},{7,6},{8,9},{9,8},{10,11... | collective-permute-start | bytes 393224 | tf_op jit(solution)/shard_map/ppermute | solution.py:267
  75.3 12.1 %collective-permute-start.11 = (bf16[128,512]{1,0:T(8,128)(2,1)S(1)}, bf16[128,512]{1,0:T(8,128)(2,1)S(1)}, u32[]{:S(2)}, u32[]{:S(2)}) collective-permute-start(bf16[128,512]{1,0:T(8,128)(2,1)S(1)} %add_convert_fusion.6), channel_id=1, source_target_pairs={{0,2},{1,3},{2,0},{3,1},{4,6},{5,7},{6,4},{7,5},{8,10},{9,11},{10,... | collective-permute-start | bytes 393224 | tf_op jit(solution)/shard_map/ppermute | solution.py:267
  78.5 10.8 %collective-permute-start.27 = (bf16[128,512]{1,0:T(8,128)(2,1)S(1)}, bf16[128,512]{1,0:T(8,128)(2,1)S(1)}, u32[]{:S(2)}, u32[]{:S(2)}) collective-permute-start(bf16[128,512]{1,0:T(8,128)(2,1)S(1)} %add_convert_fusion.4), channel_id=1, source_target_pairs={{0,2},{1,3},{2,0},{3,1},{4,6},{5,7},{6,4},{7,5},{8,10},{9,11},{10,... | collective-permute-start | bytes 393224 | tf_op jit(solution)/shard_map/ppermute | solution.py:267
  87.6 1.9 collective-permute-start.12
  89.4 12.7 %copy-start.1 = (bf16[32,64,128]{2,1,0:T(8,128)(2,1)S(1)}, bf16[32,64,128]{2,1,0:T(8,128)(2,1)}, u32[]{:S(2)}) copy-start(bf16[32,64,128]{2,1,0:T(8,128)(2,1)} %param.9) | copy-start | bytes 1572868
  89.4 17.8 %collective-permute-start.28 = (bf16[128,512]{1,0:T(8,128)(2,1)S(1)}, bf16[128,512]{1,0:T(8,128)(2,1)S(1)}, u32[]{:S(2)}, u32[]{:S(2)}) collective-permute-start(bf16[128,512]{1,0:T(8,128)(2,1)S(1)} %get-tuple-element.78.refs_0_), channel_id=1, source_target_pairs={{0,4},{4,0},{8,12},{12,8},{16,20},{20,16},{24,28},{28,24},{1,5},{5... | collective-permute-start | bytes 393224 | tf_op jit(solution)/shard_map/ppermute | solution.py:260
  100.4 18.8 %collective-permute-start.14 = (bf16[32,32,256]{2,1,0:T(8,128)(2,1)}, bf16[32,32,256]{2,1,0:T(8,128)(2,1)S(1)}, u32[]{:S(2)}, u32[]{:S(2)}) collective-permute-start(bf16[32,32,256]{2,1,0:T(8,128)(2,1)} %get-tuple-element.35), channel_id=1, source_target_pairs={{0,16},{4,12},{8,24},{12,4},{16,0},{20,28},{24,8},{28,20},{1,17},{... | collective-permute-start | bytes 1572872 | tf_op jit(solution)/shard_map/ppermute | solution.py:264
  102.1 18.9 %collective-permute-start.22 = (bf16[2,4,64,128]{3,2,1,0:T(8,128)(2,1)S(1)}, bf16[2,4,64,128]{3,2,1,0:T(8,128)(2,1)S(1)}, u32[]{:S(2)}, u32[]{:S(2)}) collective-permute-start(bf16[2,4,64,128]{3,2,1,0:T(8,128)(2,1)S(1)} %get-tuple-element.62), channel_id=1, source_target_pairs={{0,3},{1,2},{2,1},{3,0},{4,7},{5,6},{6,5},{7,4},{8,11},{9,10},{10,... | collective-permute-start | bytes 393224 | tf_op jit(solution)/shard_map/ppermute | solution.py:267
  105.4 28.7 %collective-permute-start.21 = (bf16[2,4,64,128]{3,2,1,0:T(8,128)(2,1)S(1)}, bf16[2,4,64,128]{3,2,1,0:T(8,128)(2,1)S(1)}, u32[]{:S(2)}, u32[]{:S(2)}) collective-permute-start(bf16[2,4,64,128]{3,2,1,0:T(8,128)(2,1)S(1)} %get-tuple-element.63), channel_id=1, source_target_pairs={{0,2},{1,3},{2,0},{3,1},{4,6},{5,7},{6,4},{7,5},{8,10},{9,11},{10,... | collective-permute-start | bytes 393224 | tf_op jit(solution)/shard_map/ppermute | solution.py:267
  105.4 46.9 %collective-permute-start.20 = (bf16[2,4,64,128]{3,2,1,0:T(8,128)(2,1)S(1)}, bf16[2,4,64,128]{3,2,1,0:T(8,128)(2,1)S(1)}, u32[]{:S(2)}, u32[]{:S(2)}) collective-permute-start(bf16[2,4,64,128]{3,2,1,0:T(8,128)(2,1)S(1)} %get-tuple-element.64), channel_id=1, source_target_pairs={{0,1},{1,0},{2,3},{3,2},{4,5},{5,4},{6,7},{7,6},{8,9},{9,8},{10,11... | collective-permute-start | bytes 393224 | tf_op jit(solution)/shard_map/ppermute | solution.py:267
  107.2 13.6 %copy-start.5 = (bf16[32,32,256]{2,1,0:T(8,128)(2,1)S(1)}, bf16[32,32,256]{2,1,0:T(8,128)(2,1)}, u32[]{:S(2)}) copy-start(bf16[32,32,256]{2,1,0:T(8,128)(2,1)} %get-tuple-element.34) | copy-start | bytes 1572868
  107.2 36.9 %copy-start.10 = (bf16[32,32,256]{2,1,0:T(8,128)(2,1)S(1)}, bf16[32,32,256]{2,1,0:T(8,128)(2,1)}, u32[]{:S(2)}) copy-start(bf16[32,32,256]{2,1,0:T(8,128)(2,1)} %get-tuple-element.32) | copy-start | bytes 1572868
  118.1 31.9 %copy-start.11 = (bf16[32,32,256]{2,1,0:T(8,128)(2,1)S(1)}, bf16[32,32,256]{2,1,0:T(8,128)(2,1)}, u32[]{:S(2)}) copy-start(bf16[32,32,256]{2,1,0:T(8,128)(2,1)} %get-tuple-element.40) | copy-start | bytes 1572868
  118.1 14.7 %collective-permute-start.30 = (bf16[32,32,256]{2,1,0:T(8,128)(2,1)}, bf16[32,32,256]{2,1,0:T(8,128)(2,1)S(1)}, u32[]{:S(2)}, u32[]{:S(2)}) collective-permute-start(bf16[32,32,256]{2,1,0:T(8,128)(2,1)} %get-tuple-element.43), channel_id=1, source_target_pairs={{0,16},{4,12},{8,24},{12,4},{16,0},{20,28},{24,8},{28,20},{1,17},{... | collective-permute-start | bytes 1572872 | tf_op jit(solution)/shard_map/ppermute | solution.py:264
  119.2 24.9 %collective-permute-start.13 = (bf16[32,32,256]{2,1,0:T(8,128)(2,1)S(1)}, bf16[32,32,256]{2,1,0:T(8,128)(2,1)S(1)}, u32[]{:S(2)}, u32[]{:S(2)}) collective-permute-start(bf16[32,32,256]{2,1,0:T(8,128)(2,1)S(1)} %copy-done.17), channel_id=1, source_target_pairs={{0,16},{4,12},{8,24},{12,4},{16,0},{20,28},{24,8},{28,20},{1,17},{... | collective-permute-start | bytes 1572872 | tf_op jit(solution)/shard_map/ppermute | solution.py:264
  121.0 23.1 %collective-permute-start.15 = (bf16[32,32,256]{2,1,0:T(8,128)(2,1)S(1)}, bf16[32,32,256]{2,1,0:T(8,128)(2,1)S(1)}, u32[]{:S(2)}, u32[]{:S(2)}) collective-permute-start(bf16[32,32,256]{2,1,0:T(8,128)(2,1)S(1)} %add_convert_fusion.3), channel_id=1, source_target_pairs={{0,8},{4,20},{8,0},{12,28},{16,24},{20,4},{24,16},{28,12},{1,9},{5... | collective-permute-start | bytes 1572872 | tf_op jit(solution)/shard_map/ppermute | solution.py:264
  132.9 17.2 %collective-permute-start.29 = (bf16[32,32,256]{2,1,0:T(8,128)(2,1)}, bf16[32,32,256]{2,1,0:T(8,128)(2,1)S(1)}, u32[]{:S(2)}, u32[]{:S(2)}) collective-permute-start(bf16[32,32,256]{2,1,0:T(8,128)(2,1)} %get-tuple-element.41), channel_id=1, source_target_pairs={{0,16},{4,12},{8,24},{12,4},{16,0},{20,28},{24,8},{28,20},{1,17},{... | collective-permute-start | bytes 1572872 | tf_op jit(solution)/shard_map/ppermute | solution.py:264
  134.1 15.9 %collective-permute-start.31 = (bf16[32,32,256]{2,1,0:T(8,128)(2,1)S(1)}, bf16[32,32,256]{2,1,0:T(8,128)(2,1)S(1)}, u32[]{:S(2)}, u32[]{:S(2)}) collective-permute-start(bf16[32,32,256]{2,1,0:T(8,128)(2,1)S(1)} %add_convert_fusion.1), channel_id=1, source_target_pairs={{0,8},{4,20},{8,0},{12,28},{16,24},{20,4},{24,16},{28,12},{1,9},{5... | collective-permute-start | bytes 1572872 | tf_op jit(solution)/shard_map/ppermute | solution.py:264
  144.5 6.1 %collective-permute-start.16 = (bf16[4,4,32,256]{3,2,1,0:T(8,128)(2,1)S(1)}, bf16[4,4,32,256]{3,2,1,0:T(8,128)(2,1)S(1)}, u32[]{:S(2)}, u32[]{:S(2)}) collective-permute-start(bf16[4,4,32,256]{3,2,1,0:T(8,128)(2,1)S(1)} %bitcast.110), channel_id=1, source_target_pairs={{0,4},{4,0},{8,12},{12,8},{16,20},{20,16},{24,28},{28,24},{1,5},{5... | collective-permute-start | bytes 786440 | tf_op jit(solution)/shard_map/ppermute | solution.py:260
  150.6 6.0 %collective-permute-start.32 = (bf16[4,4,32,256]{3,2,1,0:T(8,128)(2,1)S(1)}, bf16[4,4,32,256]{3,2,1,0:T(8,128)(2,1)S(1)}, u32[]{:S(2)}, u32[]{:S(2)}) collective-permute-start(bf16[4,4,32,256]{3,2,1,0:T(8,128)(2,1)S(1)} %bitcast.109), channel_id=1, source_target_pairs={{0,4},{4,0},{8,12},{12,8},{16,20},{20,16},{24,28},{28,24},{1,5},{5... | collective-permute-start | bytes 786440 | tf_op jit(solution)/shard_map/ppermute | solution.py:260
  151.4 9.7 %collective-permute-start.17 = (bf16[2,4,32,256]{3,2,1,0:T(8,128)(2,1)S(1)}, bf16[2,4,32,256]{3,2,1,0:T(8,128)(2,1)S(1)}, u32[]{:S(2)}, u32[]{:S(2)}) collective-permute-start(bf16[2,4,32,256]{3,2,1,0:T(8,128)(2,1)S(1)} %get-tuple-element.56), channel_id=1, source_target_pairs={{0,1},{1,0},{2,3},{3,2},{4,5},{5,4},{6,7},{7,6},{8,9},{9,8},{10,11... | collective-permute-start | bytes 393224 | tf_op jit(solution)/shard_map/ppermute | solution.py:267
  153.0 13.0 %collective-permute-start.18 = (bf16[2,4,32,256]{3,2,1,0:T(8,128)(2,1)S(1)}, bf16[2,4,32,256]{3,2,1,0:T(8,128)(2,1)S(1)}, u32[]{:S(2)}, u32[]{:S(2)}) collective-permute-start(bf16[2,4,32,256]{3,2,1,0:T(8,128)(2,1)S(1)} %get-tuple-element.57), channel_id=1, source_target_pairs={{0,2},{1,3},{2,0},{3,1},{4,6},{5,7},{6,4},{7,5},{8,10},{9,11},{10,... | collective-permute-start | bytes 393224 | tf_op jit(solution)/shard_map/ppermute | solution.py:267
  156.0 10.1 %collective-permute-start.19 = (bf16[2,4,32,256]{3,2,1,0:T(8,128)(2,1)S(1)}, bf16[2,4,32,256]{3,2,1,0:T(8,128)(2,1)S(1)}, u32[]{:S(2)}, u32[]{:S(2)}) collective-permute-start(bf16[2,4,32,256]{3,2,1,0:T(8,128)(2,1)S(1)} %get-tuple-element.54), channel_id=1, source_target_pairs={{0,3},{1,2},{2,1},{3,0},{4,7},{5,6},{6,5},{7,4},{8,11},{9,10},{10,... | collective-permute-start | bytes 393224 | tf_op jit(solution)/shard_map/ppermute | solution.py:267
  157.3 22.2 %collective-permute-start.33 = (bf16[2,4,32,256]{3,2,1,0:T(8,128)(2,1)S(1)}, bf16[2,4,32,256]{3,2,1,0:T(8,128)(2,1)S(1)}, u32[]{:S(2)}, u32[]{:S(2)}) collective-permute-start(bf16[2,4,32,256]{3,2,1,0:T(8,128)(2,1)S(1)} %get-tuple-element.67), channel_id=1, source_target_pairs={{0,1},{1,0},{2,3},{3,2},{4,5},{5,4},{6,7},{7,6},{8,9},{9,8},{10,11... | collective-permute-start | bytes 393224 | tf_op jit(solution)/shard_map/ppermute | solution.py:267
  157.3 23.7 %collective-permute-start.34 = (bf16[2,4,32,256]{3,2,1,0:T(8,128)(2,1)S(1)}, bf16[2,4,32,256]{3,2,1,0:T(8,128)(2,1)S(1)}, u32[]{:S(2)}, u32[]{:S(2)}) collective-permute-start(bf16[2,4,32,256]{3,2,1,0:T(8,128)(2,1)S(1)} %get-tuple-element.68), channel_id=1, source_target_pairs={{0,2},{1,3},{2,0},{3,1},{4,6},{5,7},{6,4},{7,5},{8,10},{9,11},{10,... | collective-permute-start | bytes 393224 | tf_op jit(solution)/shard_map/ppermute | solution.py:267
  161.1 19.9 %collective-permute-start.35 = (bf16[2,4,32,256]{3,2,1,0:T(8,128)(2,1)S(1)}, bf16[2,4,32,256]{3,2,1,0:T(8,128)(2,1)S(1)}, u32[]{:S(2)}, u32[]{:S(2)}) collective-permute-start(bf16[2,4,32,256]{3,2,1,0:T(8,128)(2,1)S(1)} %get-tuple-element.65), channel_id=1, source_target_pairs={{0,3},{1,2},{2,1},{3,0},{4,7},{5,6},{6,5},{7,4},{8,11},{9,10},{10,... | collective-permute-start | bytes 393224 | tf_op jit(solution)/shard_map/ppermute | solution.py:267
  169.6 19.7 %collective-permute-start.23 = (bf16[4,64,128]{2,1,0:T(8,128)(2,1)}, bf16[4,64,128]{2,1,0:T(8,128)(2,1)S(1)}, u32[]{:S(2)}, u32[]{:S(2)}) collective-permute-start(bf16[4,64,128]{2,1,0:T(8,128)(2,1)} %get-tuple-element.37), channel_id=1, source_target_pairs={{0,1},{1,0},{2,3},{3,2},{4,5},{5,4},{6,7},{7,6},{8,9},{9,8},{10,11... | collective-permute-start | bytes 196616 | tf_op jit(solution)/shard_map/ppermute | solution.py:267
  178.6 12.3 %collective-permute-start.24 = (bf16[4,64,128]{2,1,0:T(8,128)(2,1)}, bf16[4,64,128]{2,1,0:T(8,128)(2,1)S(1)}, u32[]{:S(2)}, u32[]{:S(2)}) collective-permute-start(bf16[4,64,128]{2,1,0:T(8,128)(2,1)} %get-tuple-element.38), channel_id=1, source_target_pairs={{0,2},{1,3},{2,0},{3,1},{4,6},{5,7},{6,4},{7,5},{8,10},{9,11},{10,... | collective-permute-start | bytes 196616 | tf_op jit(solution)/shard_map/ppermute | solution.py:267
  179.5 11.4 %collective-permute-start.25 = (bf16[4,64,128]{2,1,0:T(8,128)(2,1)}, bf16[4,64,128]{2,1,0:T(8,128)(2,1)S(1)}, u32[]{:S(2)}, u32[]{:S(2)}) collective-permute-start(bf16[4,64,128]{2,1,0:T(8,128)(2,1)} %get-tuple-element.39), channel_id=1, source_target_pairs={{0,3},{1,2},{2,1},{3,0},{4,7},{5,6},{6,5},{7,4},{8,11},{9,10},{10,... | collective-permute-start | bytes 196616 | tf_op jit(solution)/shard_map/ppermute | solution.py:267
  184.6 6.4 %collective-permute-start.36 = (bf16[4,64,128]{2,1,0:T(8,128)(2,1)}, bf16[4,64,128]{2,1,0:T(8,128)(2,1)S(1)}, u32[]{:S(2)}, u32[]{:S(2)}) collective-permute-start(bf16[4,64,128]{2,1,0:T(8,128)(2,1)} %get-tuple-element.45), channel_id=1, source_target_pairs={{0,1},{1,0},{2,3},{3,2},{4,5},{5,4},{6,7},{7,6},{8,9},{9,8},{10,11... | collective-permute-start | bytes 196616 | tf_op jit(solution)/shard_map/ppermute | solution.py:267
  185.6 7.4 %collective-permute-start.37 = (bf16[4,64,128]{2,1,0:T(8,128)(2,1)}, bf16[4,64,128]{2,1,0:T(8,128)(2,1)S(1)}, u32[]{:S(2)}, u32[]{:S(2)}) collective-permute-start(bf16[4,64,128]{2,1,0:T(8,128)(2,1)} %get-tuple-element.46), channel_id=1, source_target_pairs={{0,2},{1,3},{2,0},{3,1},{4,6},{5,7},{6,4},{7,5},{8,10},{9,11},{10,... | collective-permute-start | bytes 196616 | tf_op jit(solution)/shard_map/ppermute | solution.py:267
  189.3 6.3 %collective-permute-start.38 = (bf16[4,64,128]{2,1,0:T(8,128)(2,1)}, bf16[4,64,128]{2,1,0:T(8,128)(2,1)S(1)}, u32[]{:S(2)}, u32[]{:S(2)}) collective-permute-start(bf16[4,64,128]{2,1,0:T(8,128)(2,1)} %get-tuple-element.47), channel_id=1, source_target_pairs={{0,3},{1,2},{2,1},{3,0},{4,7},{5,6},{6,5},{7,4},{8,11},{9,10},{10,... | collective-permute-start | bytes 196616 | tf_op jit(solution)/shard_map/ppermute | solution.py:267
  (15 other events, 55.7 us)
where the time goes:
time: 197 us
  waiting for transfers between devices  63 us (32%)
  Pallas kernels  58.8 us (30%)
  starting transfers between devices  55.5 us (28%)
  local copies, waits for them, and re-layouts  11.5 us (6%)
  other arithmetic  6.99 us (4%)
    ppermute x12, waiting for transfers between devices, swap_chips(): return lax.ppermute(x, 'blk', pairs)  39.8 us
    ppermute x19, starting transfers between devices, swap_planes(): return lax.ppermute(x, 'rows', [(z, z ^ s) for z in range(n_rows)])  37.2 us
    pallas_call x2, Pallas kernels, potential_parts(): pl.pallas_call(functools.partial(potential_kernel, pieces=pieces, steps=s...  20.5 us
    ppermute x19, waiting for transfers between devices, swap_planes(): return lax.ppermute(x, 'rows', [(z, z ^ s) for z in range(n_rows)])  20.2 us
    pallas_call x4, Pallas kernels, vectors_inner(): pl.pallas_call(relayout_kernel, out_shape=jax.ShapeDtypeStruct((half, vec...  17.3 us
    ppermute x12, starting transfers between devices, swap_chips(): return lax.ppermute(x, 'blk', pairs)  16.9 us
    pallas_call x2, Pallas kernels, bias_parts(): pl.pallas_call(functools.partial(bias_kernel, pieces=pieces, steps=steps,...  15.2 us
    pallas_call x2, Pallas kernels, taylor_sums(): pl.pallas_call(functools.partial(taylor_kernel, groups=groups), out_shape...  5.72 us
  transfers between devices with their start and end apart: 39, of which 14 were waited for; matrix products, arithmetic and copies ran while one was open for 5% of the time, Pallas kernels for 24%

commit v1 on v0

--- a/solution.py
+++ b/solution.py
@@ -11,6 +11,8 @@
 TAYLOR = 4
 CHUNKS = 2
 PARTS = 2
+BIAS_DEPTH = 8
+DEPTH = 8
 
 time_root = 0.5
 F32, BF16 = jnp.float32, jnp.bfloat16
@@ -20,6 +22,10 @@
     if core == 0:
         return rel
     return sum(((rel >> t) & 1) << (bits - 1 - t) for t in range(bits))
+
+
+def in_hbm(arrays):
+    return [pltpu.with_memory_space_constraint(x, pltpu.HBM) for x in arrays]
 
 
 def vmem_limit():
@@ -97,7 +103,7 @@
     pieces = len(greens)
     walkers = pieces * greens[0].shape[1]
     last = part == PARTS - 1
-    depth = min(8, rows_part)
+    depth = min(BIAS_DEPTH, rows_part)
     steps = rows_part // depth
     flat = pl.BlockSpec((walkers, vecs), lambda i, o: (0, 0))
     chol_spec = pl.BlockSpec((depth, vecs, orbitals), lambda i, o: (i, 0, 0))
@@ -126,59 +132,76 @@
         ),
         compiler_params=vmem_limit(),
         name="bias",
-    )(order, *greens, kept, swapped, *before)
-
-
-def potential_kernel(order, *refs, pieces, steps):
-    shift_kept, shift_swapped = refs[:2]
-    kept, swapped = refs[2 : 2 + PARTS], refs[2 + PARTS : 2 + 2 * PARTS]
-    outs, (field,) = refs[2 + 2 * PARTS : -1], refs[-1:]
+    )(order, *in_hbm(greens), kept, swapped, *in_hbm(before))
+
+
+def potential_kernel(order, shift_kept, shift_swapped, *refs, pieces, depth, firsts):
+    kept, swapped = refs[:PARTS], refs[PARTS : 2 * PARTS]
+    outs, (field, vectors, made, arrived, left) = refs[2 * PARTS : -5], refs[-5:]
     vecs = shift_kept.shape[1]
     blocks = 2 * pieces
     rows = field.shape[0] // blocks
-
-    @pl.when(pl.program_id(0) == 0)
-    def _():
-        for b in range(blocks):
-            at = pl.ds(pl.multiple_of(order[b] * rows, rows), rows)
-            field[b * rows : (b + 1) * rows, :vecs] = shift_kept[at, :]
-            field[b * rows : (b + 1) * rows, vecs:] = shift_swapped[at, :]
-
-    for p in range(PARTS):
-
-        @pl.when(pl.program_id(0) // steps == p)
-        def _():
-            for i in range(kept[p].shape[0]):
-                vectors = jnp.concatenate([kept[p][i], swapped[p][i]], axis=0)
-                part = jnp.dot(field[...], vectors, preferred_element_type=F32).astype(BF16)
-                for j, out in enumerate(outs):
-                    out[i] = part[2 * j * rows : 2 * (j + 1) * rows]
+    per = made.shape[1] // pieces
+    steps = firsts[-1]
+
+    def fetch(step, act):
+        slot = lax.rem(step, 2)
+        for p in range(PARTS):
+
+            @pl.when((step >= firsts[p]) & (step < firsts[p + 1]))
+            def _():
+                at = pl.ds((step - firsts[p]) * depth, depth)
+                for side, source in enumerate((kept[p], swapped[p])):
+                    to = vectors.at[slot, :, side * vecs : (side + 1) * vecs]
+                    act(pltpu.make_async_copy(source.at[at], to, arrived.at[slot, side]))
+
+    fetch(0, lambda copy: copy.start())
+    for b in range(blocks):
+        at = pl.ds(pl.multiple_of(order[b] * rows, rows), rows)
+        field[b * rows : (b + 1) * rows, :vecs] = shift_kept[at, :]
+        field[b * rows : (b + 1) * rows, vecs:] = shift_swapped[at, :]
+
+    def put(step, act):
+        at = pl.ds(step * depth, depth)
+        for j, out in enumerate(outs):
+            source = made.at[at, j * per : (j + 1) * per]
+            act(pltpu.make_async_copy(source, out.at[at], left.at[step, j]))
+
+    def one(step, carry):
+        fetch(step + 1, lambda copy: copy.start())
+        fetch(step, lambda copy: copy.wait())
+        slot = lax.rem(step, 2)
+        for i in range(depth):
+            part = jnp.dot(field[...], vectors[slot, i], preferred_element_type=F32)
+            made[step * depth + i] = part.astype(BF16)
+        put(step, lambda copy: copy.start())
+        return carry
+
+    lax.fori_loop(0, steps, one, 0)
+    for step in range(steps):
+        put(step, lambda copy: copy.wait())
 
 
 def potential_parts(order, shift_kept, shift_swapped, kept, swapped, pieces):
-    rows_part, vecs, orbitals = kept[0].shape
-    rows = PARTS * rows_part
+    vecs, orbitals = kept[0].shape[1:]
     walkers = shift_kept.shape[0]
-    depth = min(8, rows_part)
-    steps = rows_part // depth
-    chol_specs = [
-        pl.BlockSpec(
-            (depth, vecs, orbitals), lambda i, o, p=p: (jnp.clip(i - p * steps, 0, steps - 1), 0, 0)
-        )
-        for p in range(PARTS)
-    ]
-    shift_spec = pl.BlockSpec((walkers, vecs), lambda i, o: (0, 0))
+    depth = min(DEPTH, min(x.shape[0] for x in kept))
+    firsts = [sum(x.shape[0] for x in kept[:p]) // depth for p in range(PARTS + 1)]
+    rows = firsts[-1] * depth
+    vmem, hbm = pl.BlockSpec(memory_space=pltpu.VMEM), pl.BlockSpec(memory_space=pl.ANY)
     per = walkers // pieces
     return pl.pallas_call(
-        functools.partial(potential_kernel, pieces=pieces, steps=steps),
+        functools.partial(potential_kernel, pieces=pieces, depth=depth, firsts=firsts),
         out_shape=[jax.ShapeDtypeStruct((rows, per, orbitals), BF16)] * pieces,
-        grid_spec=pltpu.PrefetchScalarGridSpec(
-            num_scalar_prefetch=1,
-            grid=(rows // depth,),
-            in_specs=[shift_spec] * 2 + chol_specs * 2,
-            out_specs=[pl.BlockSpec((depth, per, orbitals), lambda i, o: (i, 0, 0))] * pieces,
-            scratch_shapes=[pltpu.VMEM((walkers, 2 * vecs), BF16)],
-        ),
+        in_specs=[pl.BlockSpec(memory_space=pltpu.SMEM)] + [vmem] * 2 + [hbm] * (2 * PARTS),
+        out_specs=[hbm] * pieces,
+        scratch_shapes=[
+            pltpu.VMEM((walkers, 2 * vecs), BF16),
+            pltpu.VMEM((2, depth, 2 * vecs, orbitals), BF16),
+            pltpu.VMEM((rows, walkers, orbitals), BF16),
+            pltpu.SemaphoreType.DMA((2, 2)),
+            pltpu.SemaphoreType.DMA((rows // depth, pieces)),
+        ],
         cost_estimate=pl.CostEstimate(
             flops=4 * walkers * rows * vecs * orbitals,
             bytes_accessed=4 * rows * vecs * orbitals + 2 * walkers * rows * orbitals,
@@ -194,14 +217,14 @@
     outs = refs[2 * groups : 3 * groups]
     full_pot, full_term, full_sum = refs[3 * groups :]
     low = pots[0].shape[2]
-    high = terms[0].shape[1]
+    high = terms[0].shape[2]
     for s, piece in enumerate(pots):
         for h in range(2):
             at = pl.ds(pl.multiple_of(order[2 * s + h] * low, low), low)
             full_pot[:, at, :] = piece[h]
     for s, piece in enumerate(terms):
         at = pl.ds(pl.multiple_of((order[2 * s] // 2) * high, high), high)
-        full_term[:, at, :] = piece[...]
+        full_term[:, at, :] = piece[0]
     count = full_pot.shape[0]
     now = [full_term[w] for w in range(count)]
     total = [None] * count
@@ -218,16 +241,21 @@
         out[...] = full_sum[:, at, :]
 
 
-def taylor_sums(order, pots, terms):
+def taylor_sums(order, chunk, pots, terms):
     groups = len(terms)
-    _, count, _, orbitals = pots[0].shape
-    high, occupied = terms[0].shape[1:]
-    vmem = pl.BlockSpec(memory_space=pltpu.VMEM)
+    _, count, low, orbitals = pots[0].shape
+    _, _, high, occupied = terms[0].shape
+    pot_spec = pl.BlockSpec((2, count, low, orbitals), lambda i: (0, 0, 0, 0))
+    term_spec = pl.BlockSpec((1, count, high, occupied), lambda i: (chunk, 0, 0, 0))
+    out_spec = pl.BlockSpec((count, high, occupied), lambda i: (0, 0, 0))
     return pl.pallas_call(
         functools.partial(taylor_kernel, groups=groups),
         out_shape=[jax.ShapeDtypeStruct((count, high, occupied), BF16)] * groups,
-        in_specs=[pl.BlockSpec(memory_space=pltpu.SMEM)] + [vmem] * (2 * groups),
-        out_specs=[vmem] * groups,
+        grid=(1,),
+        in_specs=[pl.BlockSpec(memory_space=pltpu.SMEM)]
+        + [pot_spec] * groups
+        + [term_spec] * groups,
+        out_specs=[out_spec] * groups,
         scratch_shapes=[
             pltpu.VMEM((count, orbitals, orbitals), BF16),
             pltpu.VMEM((count, orbitals, occupied), BF16),
@@ -240,7 +268,7 @@
         ),
         compiler_params=vmem_limit(),
         name="taylor",
-    )(order, *pots, *terms)
+    )(order, *in_hbm(pots), *in_hbm(terms))
 
 
 def propagate(cholesky, green, aux_field, walker_orbitals):
@@ -331,7 +359,7 @@
             lax.dynamic_index_in_dim(sides, plane ^ s, 1, keepdims=False) for s in range(n_rows)
         ]
         pots = [swap_planes(p, s) if s else p for s, p in enumerate(pots)]
-        sums = taylor_sums(plane_order, pots, [t[c] for t in terms])
+        sums = taylor_sums(plane_order, c, pots, terms)
         result = jnp.zeros((n_rows, each, rows_dev, occupied), BF16)
         for s in range(n_rows):
             got = swap_planes(sums[s], s) if s else sums[s]

time: 197 us -> 200 us (1.015)
  other arithmetic: 6.99 us -> 10.3 us
    squeeze x4 -> x0, local copies, waits for them, and re-layouts: 2.63 us -> none  [propagated(): sums = taylor_sums(plane_order, pots, [t[c] for t in terms])]
    transpose x2, other arithmetic: 0.55 us -> 2.94 us  [scatter_potential(): potential = total[0].astype(BF16).transpose(1, 0, 2)]
    unnamed x50 -> x54, local copies, waits for them, and re-layouts: 4.27 us -> 4.29 us
  transfers between devices with their start and end apart: 39 -> 39, of which waited for: 14 -> 16; matrix products, arithmetic and copies ran while one was open for 5% -> 6% of each run, Pallas kernels for 24% -> 22%
where the time goes in v1:
time: 200 us
  waiting for transfers between devices  64.3 us (32%)
  Pallas kernels  57.4 us (29%)
  starting transfers between devices  57.2 us (29%)
  other arithmetic  10.3 us (5%)
  local copies, waits for them, and re-layouts  9.52 us (5%)
    ppermute x12, waiting for transfers between devices, swap_chips(): return lax.ppermute(x, 'blk', pairs)  40.6 us
    ppermute x19, starting transfers between devices, swap_planes(): return lax.ppermute(x, 'rows', [(z, z ^ s) for z in range(n_rows)])  38.9 us
    ppermute x19, waiting for transfers between devices, swap_planes(): return lax.ppermute(x, 'rows', [(z, z ^ s) for z in range(n_rows)])  19.4 us
    pallas_call x2, Pallas kernels, potential_parts(): pl.pallas_call(functools.partial(potential_kernel, pieces=pieces, depth=d...  19.2 us
    pallas_call x4, Pallas kernels, vectors_inner(): pl.pallas_call(relayout_kernel, out_shape=jax.ShapeDtypeStruct((half, vec...  17.2 us
    ppermute x12, starting transfers between devices, swap_chips(): return lax.ppermute(x, 'blk', pairs)  16.9 us
    pallas_call x2, Pallas kernels, bias_parts(): pl.pallas_call(functools.partial(bias_kernel, pieces=pieces, steps=steps,...  15.3 us
    pallas_call x2, Pallas kernels, taylor_sums(): pl.pallas_call(functools.partial(taylor_kernel, groups=groups), out_shape...  5.7 us
  transfers between devices with their start and end apart: 39, of which 16 were waited for; matrix products, arithmetic and copies ran while one was open for 6% of the time, Pallas kernels for 22%

profile of v1, /device:TPU:0, one launch (start us, length us, event | category | flops | bytes accessed | tf_op | source)
XLA Modules:
  0.0 199.9 jit_solution(1989386695359501328)
XLA Ops:
  0.6 1.3 constant_dynamic-slice_fusion.1
  4.5 4.6 %relayout.7 = bf16[16,512,256]{2,1,0:T(8,128)(2,1)} custom-call(s32[1]{0:T(128)} %bitcast.7.which, bf16[512,64,256]{2,1,0:T(8,128)(2,1)} %block.3), custom_call_target="tpu_custom_call" | custom-call | bytes 8388608 | tf_op jit(solution)/shard_map/relayout/pallas_call | solution.py:44
  9.4 4.2 %relayout.5 = bf16[16,512,256]{2,1,0:T(8,128)(2,1)} custom-call(s32[1]{0:T(128)} %bitcast.5.which, bf16[512,64,256]{2,1,0:T(8,128)(2,1)} %block.3), custom_call_target="tpu_custom_call" | custom-call | bytes 8388608 | tf_op jit(solution)/shard_map/relayout/pallas_call | solution.py:44
  13.8 2.8 %collective-permute-start.5 = (bf16[16,64,256]{2,1,0:T(8,128)(2,1)S(1)}, bf16[16,64,256]{2,1,0:T(8,128)(2,1)S(1)}, u32[]{:S(2)}, u32[]{:S(2)}) collective-permute-start(bf16[16,64,256]{2,1,0:T(8,128)(2,1)S(1)} %get-tuple-element.27.refs_0_), channel_id=1, source_target_pairs={{0,8},{4,20},{8,0},{12,28},{16,24},{20,4},{24,16},{28,12},{1,9},{5... | collective-permute-start | bytes 1572872 | tf_op jit(solution)/shard_map/ppermute | solution.py:292
  16.6 1.5 collective-permute-start.6
  18.7 9.8 %collective-permute-done.5.refs_1_ = bf16[16,64,256]{2,1,0:T(8,128)(2,1)S(1)} collective-permute-done((bf16[16,64,256]{2,1,0:T(8,128)(2,1)S(1)}, bf16[16,64,256]{2,1,0:T(8,128)(2,1)S(1)}, u32[]{:S(2)}, u32[]{:S(2)}) %collective-permute-start.5) | collective-permute-done | bytes 524320 | tf_op jit(solution)/shard_map/ppermute | solution.py:292
  28.5 2.1 %collective-permute-start.7 = (bf16[16,64,256]{2,1,0:T(8,128)(2,1)S(1)}, bf16[16,64,256]{2,1,0:T(8,128)(2,1)}, u32[]{:S(2)}, u32[]{:S(2)}) collective-permute-start(bf16[16,64,256]{2,1,0:T(8,128)(2,1)S(1)} %collective-permute-done.5.refs_1_), channel_id=1, source_target_pairs={{0,16},{4,12},{8,24},{12,4},{16,0},{20,28},{24,8},{28,20},{1,17},{... | collective-permute-start | bytes 1572872 | tf_op jit(solution)/shard_map/ppermute | solution.py:292
  31.4 1.5 collective-permute-start.2
  32.9 6.4 %collective-permute-done.1.refs_1_ = bf16[16,64,256]{2,1,0:T(8,128)(2,1)S(1)} collective-permute-done((bf16[16,64,256]{2,1,0:T(8,128)(2,1)S(1)}, bf16[16,64,256]{2,1,0:T(8,128)(2,1)S(1)}, u32[]{:S(2)}, u32[]{:S(2)}) %collective-permute-start.1) | collective-permute-done | bytes 524320 | tf_op jit(solution)/shard_map/ppermute | solution.py:292
  39.3 1.4 collective-permute-start.3
  41.3 4.3 %relayout.6.refs_4_.refs_0_ = bf16[16,512,256]{2,1,0:T(8,128)(2,1)} custom-call(s32[1]{0:T(128)} %bitcast.6.which, bf16[512,64,256]{2,1,0:T(8,128)(2,1)} %block.3), custom_call_target="tpu_custom_call" | custom-call | bytes 8388608 | tf_op jit(solution)/shard_map/relayout/pallas_call | solution.py:44
  45.5 4.2 %relayout.4.refs_4_.refs_1_ = bf16[16,512,256]{2,1,0:T(8,128)(2,1)} custom-call(s32[1]{0:T(128)} %bitcast.4.which, bf16[512,64,256]{2,1,0:T(8,128)(2,1)} %block.3), custom_call_target="tpu_custom_call" | custom-call | bytes 8388608 | tf_op jit(solution)/shard_map/relayout/pallas_call | solution.py:44
  49.8 7.4 %bias.2 = (f32[256,512]{1,0:T(8,128)}, f32[256,512]{1,0:T(8,128)}) custom-call(s32[8]{0:T(128)} %fusion.24.order, bf16[16,64,256]{2,1,0:T(8,128)(2,1)} %copy-done.2, bf16[16,64,256]{2,1,0:T(8,128)(2,1)} %copy-done.15, bf16[16,64,256]{2,1,0:T(8,128)(2,1)} %copy-done.16, bf16[16,64,256]{2,1,0:T(8,128)(2,1)} %collective-permute-done.7.refs_3_, ...), custom_call_target="tpu_custom_call" | custom-call | flops 2147483648 | bytes 10485760 | tf_op jit(solution)/shard_map/bias/pallas_call | solution.py:114
  58.1 7.9 %bias.3 = (f32[2,128,512]{2,1,0:T(8,128)}, bf16[2,128,512]{2,1,0:T(8,128)(2,1)}) custom-call(s32[8]{0:T(128)} %fusion.24.order, bf16[16,64,256]{2,1,0:T(8,128)(2,1)} %copy-done, bf16[16,64,256]{2,1,0:T(8,128)(2,1)} %copy-done.5, bf16[16,64,256]{2,1,0:T(8,128)(2,1)} %copy-done.7, bf16[16,64,256]{2,1,0:T(8,128)(2,1)} %copy-done.8, ...), custom_call_target="tpu_custom_call" | custom-call | flops 2147483648 | bytes 10485760 | tf_op jit(solution)/shard_map/bias/pallas_call | solution.py:114
  66.0 1.7 collective-permute-done.9
  68.9 2.1 %collective-permute-start.10 = (bf16[128,512]{1,0:T(8,128)(2,1)S(1)}, bf16[128,512]{1,0:T(8,128)(2,1)S(1)}, u32[]{:S(2)}, u32[]{:S(2)}) collective-permute-start(bf16[128,512]{1,0:T(8,128)(2,1)S(1)} %get-tuple-element.50), channel_id=1, source_target_pairs={{0,1},{1,0},{2,3},{3,2},{4,5},{5,4},{6,7},{7,6},{8,9},{9,8},{10,11... | collective-permute-start | bytes 393224 | tf_op jit(solution)/shard_map/ppermute | solution.py:295
  70.9 3.8 %collective-permute-done.10 = bf16[128,512]{1,0:T(8,128)(2,1)S(1)} collective-permute-done((bf16[128,512]{1,0:T(8,128)(2,1)S(1)}, bf16[128,512]{1,0:T(8,128)(2,1)S(1)}, u32[]{:S(2)}, u32[]{:S(2)}) %collective-permute-start.10) | collective-permute-done | bytes 131104 | tf_op jit(solution)/shard_map/ppermute | solution.py:295
  74.8 2.8 %collective-permute-start.11 = (bf16[128,512]{1,0:T(8,128)(2,1)S(1)}, bf16[128,512]{1,0:T(8,128)(2,1)S(1)}, u32[]{:S(2)}, u32[]{:S(2)}) collective-permute-start(bf16[128,512]{1,0:T(8,128)(2,1)S(1)} %add_convert_fusion.6), channel_id=1, source_target_pairs={{0,2},{1,3},{2,0},{3,1},{4,6},{5,7},{6,4},{7,5},{8,10},{9,11},{10,... | collective-permute-start | bytes 393224 | tf_op jit(solution)/shard_map/ppermute | solution.py:295
  77.6 1.6 collective-permute-start.26
  79.3 4.2 %collective-permute-done.11 = bf16[128,512]{1,0:T(8,128)(2,1)S(1)} collective-permute-done((bf16[128,512]{1,0:T(8,128)(2,1)S(1)}, bf16[128,512]{1,0:T(8,128)(2,1)S(1)}, u32[]{:S(2)}, u32[]{:S(2)}) %collective-permute-start.11) | collective-permute-done | bytes 131104 | tf_op jit(solution)/shard_map/ppermute | solution.py:295
  85.8 9.6 %potential.2 = (bf16[32,32,256]{2,1,0:T(8,128)(2,1)}, bf16[32,32,256]{2,1,0:T(8,128)(2,1)}, bf16[32,32,256]{2,1,0:T(8,128)(2,1)}, bf16[32,32,256]{2,1,0:T(8,128)(2,1)}) custom-call(s32[8]{0:T(128)} %fusion.24.order, bf16[128,512]{1,0:T(8,128)(2,1)} %copy-done.3, bf16[128,512]{1,0:T(8,128)(2,1)} %copy-done.17, bf16[16,512,256]{2,1,0:T(8,128)(2,1)} %relayout.6.refs_4_.refs_0_, ...), custom_call_target="tpu_custom_call" | custom-call | flops 2147483648 | bytes 18874368 | tf_op jit(solution)/shard_map/potential/pallas_call | solution.py:193
  95.4 1.6 collective-permute-start.14
  97.2 1.3 collective-permute-done.28.shift_swapped
  99.2 9.6 %potential.3 = (bf16[32,32,256]{2,1,0:T(8,128)(2,1)}, bf16[32,32,256]{2,1,0:T(8,128)(2,1)}, bf16[32,32,256]{2,1,0:T(8,128)(2,1)}, bf16[32,32,256]{2,1,0:T(8,128)(2,1)}) custom-call(s32[8]{0:T(128)} %fusion.24.order, bf16[128,512]{1,0:T(8,128)(2,1)} %copy-done.4, bf16[128,512]{1,0:T(8,128)(2,1)} %copy-done.18, bf16[16,512,256]{2,1,0:T(8,128)(2,1)} %relayout.6.refs_4_.refs_0_, ...), custom_call_target="tpu_custom_call" | custom-call | flops 2147483648 | bytes 18874368 | tf_op jit(solution)/shard_map/potential/pallas_call | solution.py:193
  109.7 1.3 collective-permute-start.13
  111.1 1.5 collective-permute-start.15
  112.9 10.3 %collective-permute-done.30 = bf16[32,32,256]{2,1,0:T(8,128)(2,1)S(1)} collective-permute-done((bf16[32,32,256]{2,1,0:T(8,128)(2,1)}, bf16[32,32,256]{2,1,0:T(8,128)(2,1)S(1)}, u32[]{:S(2)}, u32[]{:S(2)}) %collective-permute-start.30) | collective-permute-done | bytes 524320 | tf_op jit(solution)/shard_map/ppermute | solution.py:292
  123.2 1.3 add_convert_fusion.1
  124.5 1.5 collective-permute-start.31
  125.9 8.6 %collective-permute-done.13 = bf16[32,32,256]{2,1,0:T(8,128)(2,1)} collective-permute-done((bf16[32,32,256]{2,1,0:T(8,128)(2,1)}, bf16[32,32,256]{2,1,0:T(8,128)(2,1)}, u32[]{:S(2)}, u32[]{:S(2)}) %collective-permute-start.13) | collective-permute-done | bytes 524320 | tf_op jit(solution)/shard_map/ppermute | solution.py:292
  134.5 1.5 fusion
  136.2 4.6 %collective-permute-done.29 = bf16[32,32,256]{2,1,0:T(8,128)(2,1)} collective-permute-done((bf16[32,32,256]{2,1,0:T(8,128)(2,1)}, bf16[32,32,256]{2,1,0:T(8,128)(2,1)}, u32[]{:S(2)}, u32[]{:S(2)}) %collective-permute-start.29) | collective-permute-done | bytes 524320 | tf_op jit(solution)/shard_map/ppermute | solution.py:292
  140.9 1.5 fusion.1
  143.3 2.6 %collective-permute-start.20 = (bf16[2,4,64,128]{3,2,1,0:T(8,128)(2,1)S(1)}, bf16[2,4,64,128]{3,2,1,0:T(8,128)(2,1)S(1)}, u32[]{:S(2)}, u32[]{:S(2)}) collective-permute-start(bf16[2,4,64,128]{3,2,1,0:T(8,128)(2,1)S(1)} %get-tuple-element.62), channel_id=1, source_target_pairs={{0,1},{1,0},{2,3},{3,2},{4,5},{5,4},{6,7},{7,6},{8,9},{9,8},{10,11... | collective-permute-start | bytes 393224 | tf_op jit(solution)/shard_map/ppermute | solution.py:295
  148.3 1.6 fusion.17
  151.7 2.2 %collective-permute-start.18 = (bf16[2,4,32,256]{3,2,1,0:T(8,128)(2,1)S(1)}, bf16[2,4,32,256]{3,2,1,0:T(8,128)(2,1)S(1)}, u32[]{:S(2)}, u32[]{:S(2)}) collective-permute-start(bf16[2,4,32,256]{3,2,1,0:T(8,128)(2,1)S(1)} %get-tuple-element.55), channel_id=1, source_target_pairs={{0,2},{1,3},{2,0},{3,1},{4,6},{5,7},{6,4},{7,5},{8,10},{9,11},{10,... | collective-permute-start | bytes 393224 | tf_op jit(solution)/shard_map/ppermute | solution.py:295
  153.9 1.4 collective-permute-start.19
  156.1 2.7 %collective-permute-done.21.refs_6_ = bf16[2,4,64,128]{3,2,1,0:T(8,128)(2,1)S(1)} collective-permute-done((bf16[2,4,64,128]{3,2,1,0:T(8,128)(2,1)S(1)}, bf16[2,4,64,128]{3,2,1,0:T(8,128)(2,1)S(1)}, u32[]{:S(2)}, u32[]{:S(2)}) %collective-permute-start.21) | collective-permute-done | bytes 131104 | tf_op jit(solution)/shard_map/ppermute | solution.py:295
  158.8 8.0 %collective-permute-start.34 = (bf16[2,4,32,256]{3,2,1,0:T(8,128)(2,1)S(1)}, bf16[2,4,32,256]{3,2,1,0:T(8,128)(2,1)S(1)}, u32[]{:S(2)}, u32[]{:S(2)}) collective-permute-start(bf16[2,4,32,256]{3,2,1,0:T(8,128)(2,1)S(1)} %get-tuple-element.67), channel_id=1, source_target_pairs={{0,2},{1,3},{2,0},{3,1},{4,6},{5,7},{6,4},{7,5},{8,10},{9,11},{10,... | collective-permute-start | bytes 393224 | tf_op jit(solution)/shard_map/ppermute | solution.py:295
  166.9 3.3 %collective-permute-start.35 = (bf16[2,4,32,256]{3,2,1,0:T(8,128)(2,1)S(1)}, bf16[2,4,32,256]{3,2,1,0:T(8,128)(2,1)S(1)}, u32[]{:S(2)}, u32[]{:S(2)}) collective-permute-start(bf16[2,4,32,256]{3,2,1,0:T(8,128)(2,1)S(1)} %get-tuple-element.64), channel_id=1, source_target_pairs={{0,3},{1,2},{2,1},{3,0},{4,7},{5,6},{6,5},{7,4},{8,11},{9,10},{10,... | collective-permute-start | bytes 393224 | tf_op jit(solution)/shard_map/ppermute | solution.py:295
  171.0 4.6 %collective-permute-done.18.refs_2_ = bf16[2,4,32,256]{3,2,1,0:T(8,128)(2,1)S(1)} collective-permute-done((bf16[2,4,32,256]{3,2,1,0:T(8,128)(2,1)S(1)}, bf16[2,4,32,256]{3,2,1,0:T(8,128)(2,1)S(1)}, u32[]{:S(2)}, u32[]{:S(2)}) %collective-permute-start.18) | collective-permute-done | bytes 131104 | tf_op jit(solution)/shard_map/ppermute | solution.py:295
  176.4 2.8 %taylor.2 = (bf16[4,64,128]{2,1,0:T(8,128)(2,1)}, bf16[4,64,128]{2,1,0:T(8,128)(2,1)}, bf16[4,64,128]{2,1,0:T(8,128)(2,1)}, bf16[4,64,128]{2,1,0:T(8,128)(2,1)}) custom-call(s32[8]{0:T(128)} %iota_xor_fusion.order, bf16[2,4,32,256]{3,2,1,0:T(8,128)(2,1)} %get-tuple-element.53.refs_0_, bf16[2,4,32,256]{3,2,1,0:T(8,128)(2,1)} %copy-done.20, ...), custom_call_target="tpu_custom_call" | custom-call | flops 268435456 | bytes 1048576 | tf_op jit(solution)/shard_map/taylor/pallas_call | solution.py:251
  179.2 3.3 %collective-permute-start.23 = (bf16[4,64,128]{2,1,0:T(8,128)(2,1)}, bf16[4,64,128]{2,1,0:T(8,128)(2,1)S(1)}, u32[]{:S(2)}, u32[]{:S(2)}) collective-permute-start(bf16[4,64,128]{2,1,0:T(8,128)(2,1)} %get-tuple-element.37), channel_id=1, source_target_pairs={{0,1},{1,0},{2,3},{3,2},{4,5},{5,4},{6,7},{7,6},{8,9},{9,8},{10,11... | collective-permute-start | bytes 196616 | tf_op jit(solution)/shard_map/ppermute | solution.py:295
  182.5 2.4 %collective-permute-start.25 = (bf16[4,64,128]{2,1,0:T(8,128)(2,1)}, bf16[4,64,128]{2,1,0:T(8,128)(2,1)S(1)}, u32[]{:S(2)}, u32[]{:S(2)}) collective-permute-start(bf16[4,64,128]{2,1,0:T(8,128)(2,1)} %get-tuple-element.39), channel_id=1, source_target_pairs={{0,3},{1,2},{2,1},{3,0},{4,7},{5,6},{6,5},{7,4},{8,11},{9,10},{10,... | collective-permute-start | bytes 196616 | tf_op jit(solution)/shard_map/ppermute | solution.py:295
  185.7 2.9 %taylor.3 = (bf16[4,64,128]{2,1,0:T(8,128)(2,1)}, bf16[4,64,128]{2,1,0:T(8,128)(2,1)}, bf16[4,64,128]{2,1,0:T(8,128)(2,1)}, bf16[4,64,128]{2,1,0:T(8,128)(2,1)}) custom-call(s32[8]{0:T(128)} %iota_xor_fusion.order, bf16[2,4,32,256]{3,2,1,0:T(8,128)(2,1)} %get-tuple-element.65.refs_0_, bf16[2,4,32,256]{3,2,1,0:T(8,128)(2,1)} %copy-done.19, ...), custom_call_target="tpu_custom_call" | custom-call | flops 268435456 | bytes 1048576 | tf_op jit(solution)/shard_map/taylor/pallas_call | solution.py:251
  192.4 2.4 %collective-permute-start.38 = (bf16[4,64,128]{2,1,0:T(8,128)(2,1)}, bf16[4,64,128]{2,1,0:T(8,128)(2,1)S(1)}, u32[]{:S(2)}, u32[]{:S(2)}) collective-permute-start(bf16[4,64,128]{2,1,0:T(8,128)(2,1)} %get-tuple-element.47), channel_id=1, source_target_pairs={{0,3},{1,2},{2,1},{3,0},{4,7},{5,6},{6,5},{7,4},{8,11},{9,10},{10,... | collective-permute-start | bytes 196616 | tf_op jit(solution)/shard_map/ppermute | solution.py:295
  194.9 1.4 collective-permute-done.37
  196.4 2.3 %collective-permute-done.38 = bf16[4,64,128]{2,1,0:T(8,128)(2,1)S(1)} collective-permute-done((bf16[4,64,128]{2,1,0:T(8,128)(2,1)}, bf16[4,64,128]{2,1,0:T(8,128)(2,1)S(1)}, u32[]{:S(2)}, u32[]{:S(2)}) %collective-permute-start.38) | collective-permute-done | bytes 65568 | tf_op jit(solution)/shard_map/ppermute | solution.py:295
  (132 shorter events, 24.7 us)
Async XLA Ops:
  2.2 2.1 %collective-permute-start = (bf16[32,32,256]{2,1,0:T(8,128)(2,1)S(1)}, bf16[32,32,256]{2,1,0:T(8,128)(2,1)S(1)}, u32[]{:S(2)}, u32[]{:S(2)}) collective-permute-start(bf16[32,32,256]{2,1,0:T(8,128)(2,1)S(1)} %bitcast.101), channel_id=1, source_target_pairs={{0,4},{4,0},{8,12},{12,8},{16,20},{20,16},{24,28},{28,24},{1,5},{5... | collective-permute-start | bytes 1572872 | tf_op jit(solution)/shard_map/ppermute | solution.py:288
  4.5 26.9 %copy-start = (bf16[16,64,256]{2,1,0:T(8,128)(2,1)}, bf16[16,64,256]{2,1,0:T(8,128)(2,1)S(1)}, u32[]{:S(2)}) copy-start(bf16[16,64,256]{2,1,0:T(8,128)(2,1)S(1)} %get-tuple-element.25.refs_0_) | copy-start | bytes 1572868
  9.0 40.7 %collective-permute-start.8 = (bf16[16,512,256]{2,1,0:T(8,128)(2,1)}, bf16[16,512,256]{2,1,0:T(8,128)(2,1)}, u32[]{:S(2)}, u32[]{:S(2)}) collective-permute-start(bf16[16,512,256]{2,1,0:T(8,128)(2,1)} %relayout.7), channel_id=1, source_target_pairs={{0,4},{4,0},{8,12},{12,8},{16,20},{20,16},{24,28},{28,24},{1,5},{5... | collective-permute-start | bytes 12582920 | tf_op jit(solution)/shard_map/ppermute | solution.py:288
  9.4 31.4 %copy-start.25 = (s32[8]{0:T(128)S(1)}, s32[8]{0:T(128)}, u32[]{:S(2)}) copy-start(s32[8]{0:T(128)} %constant.76.clone) | copy-start | bytes 100
  13.6 43.5 %collective-permute-start.4 = (bf16[16,512,256]{2,1,0:T(8,128)(2,1)}, bf16[16,512,256]{2,1,0:T(8,128)(2,1)}, u32[]{:S(2)}, u32[]{:S(2)}) collective-permute-start(bf16[16,512,256]{2,1,0:T(8,128)(2,1)} %relayout.5), channel_id=1, source_target_pairs={{0,4},{4,0},{8,12},{12,8},{16,20},{20,16},{24,28},{28,24},{1,5},{5... | collective-permute-start | bytes 12582920 | tf_op jit(solution)/shard_map/ppermute | solution.py:288
  13.8 14.8 %collective-permute-start.5 = (bf16[16,64,256]{2,1,0:T(8,128)(2,1)S(1)}, bf16[16,64,256]{2,1,0:T(8,128)(2,1)S(1)}, u32[]{:S(2)}, u32[]{:S(2)}) collective-permute-start(bf16[16,64,256]{2,1,0:T(8,128)(2,1)S(1)} %get-tuple-element.27.refs_0_), channel_id=1, source_target_pairs={{0,8},{4,20},{8,0},{12,28},{16,24},{20,4},{24,16},{28,12},{1,9},{5... | collective-permute-start | bytes 1572872 | tf_op jit(solution)/shard_map/ppermute | solution.py:292
  16.6 14.8 %collective-permute-start.6 = (bf16[16,64,256]{2,1,0:T(8,128)(2,1)S(1)}, bf16[16,64,256]{2,1,0:T(8,128)(2,1)S(1)}, u32[]{:S(2)}, u32[]{:S(2)}) collective-permute-start(bf16[16,64,256]{2,1,0:T(8,128)(2,1)S(1)} %get-tuple-element.27.refs_0_), channel_id=1, source_target_pairs={{0,16},{4,12},{8,24},{12,4},{16,0},{20,28},{24,8},{28,20},{1,17},{... | collective-permute-start | bytes 1572872 | tf_op jit(solution)/shard_map/ppermute | solution.py:292
  18.1 21.2 %collective-permute-start.1 = (bf16[16,64,256]{2,1,0:T(8,128)(2,1)S(1)}, bf16[16,64,256]{2,1,0:T(8,128)(2,1)S(1)}, u32[]{:S(2)}, u32[]{:S(2)}) collective-permute-start(bf16[16,64,256]{2,1,0:T(8,128)(2,1)S(1)} %get-tuple-element.25.refs_0_), channel_id=1, source_target_pairs={{0,8},{4,20},{8,0},{12,28},{16,24},{20,4},{24,16},{28,12},{1,9},{5... | collective-permute-start | bytes 1572872 | tf_op jit(solution)/shard_map/ppermute | solution.py:292
  28.5 17.0 %copy-start.15 = (bf16[16,64,256]{2,1,0:T(8,128)(2,1)}, bf16[16,64,256]{2,1,0:T(8,128)(2,1)S(1)}, u32[]{:S(2)}) copy-start(bf16[16,64,256]{2,1,0:T(8,128)(2,1)S(1)} %collective-permute-done.5.refs_1_) | copy-start | bytes 1572868
  28.5 21.2 %collective-permute-start.7 = (bf16[16,64,256]{2,1,0:T(8,128)(2,1)S(1)}, bf16[16,64,256]{2,1,0:T(8,128)(2,1)}, u32[]{:S(2)}, u32[]{:S(2)}) collective-permute-start(bf16[16,64,256]{2,1,0:T(8,128)(2,1)S(1)} %collective-permute-done.5.refs_1_), channel_id=1, source_target_pairs={{0,16},{4,12},{8,24},{12,4},{16,0},{20,28},{24,8},{28,20},{1,17},{... | collective-permute-start | bytes 1572872 | tf_op jit(solution)/shard_map/ppermute | solution.py:292
  31.4 25.7 %collective-permute-start.2 = (bf16[16,64,256]{2,1,0:T(8,128)(2,1)S(1)}, bf16[16,64,256]{2,1,0:T(8,128)(2,1)S(1)}, u32[]{:S(2)}, u32[]{:S(2)}) collective-permute-start(bf16[16,64,256]{2,1,0:T(8,128)(2,1)S(1)} %get-tuple-element.25.refs_0_), channel_id=1, source_target_pairs={{0,16},{4,12},{8,24},{12,4},{16,0},{20,28},{24,8},{28,20},{1,17},{... | collective-permute-start | bytes 1572872 | tf_op jit(solution)/shard_map/ppermute | solution.py:292
  39.3 17.8 %collective-permute-start.3 = (bf16[16,64,256]{2,1,0:T(8,128)(2,1)S(1)}, bf16[16,64,256]{2,1,0:T(8,128)(2,1)S(1)}, u32[]{:S(2)}, u32[]{:S(2)}) collective-permute-start(bf16[16,64,256]{2,1,0:T(8,128)(2,1)S(1)} %collective-permute-done.1.refs_1_), channel_id=1, source_target_pairs={{0,16},{4,12},{8,24},{12,4},{16,0},{20,28},{24,8},{28,20},{1,17},{... | collective-permute-start | bytes 1572872 | tf_op jit(solution)/shard_map/ppermute | solution.py:292
  58.1 19.5 %copy-start.9 = (f32[256,512]{1,0:T(8,128)S(1)}, f32[256,512]{1,0:T(8,128)}, u32[]{:S(2)}) copy-start(f32[256,512]{1,0:T(8,128)} %param.8) | copy-start | bytes 1572868
  66.0 1.7 collective-permute-start.9
  68.9 5.9 %collective-permute-start.10 = (bf16[128,512]{1,0:T(8,128)(2,1)S(1)}, bf16[128,512]{1,0:T(8,128)(2,1)S(1)}, u32[]{:S(2)}, u32[]{:S(2)}) collective-permute-start(bf16[128,512]{1,0:T(8,128)(2,1)S(1)} %get-tuple-element.50), channel_id=1, source_target_pairs={{0,1},{1,0},{2,3},{3,2},{4,5},{5,4},{6,7},{7,6},{8,9},{9,8},{10,11... | collective-permute-start | bytes 393224 | tf_op jit(solution)/shard_map/ppermute | solution.py:295
  74.8 8.7 %collective-permute-start.11 = (bf16[128,512]{1,0:T(8,128)(2,1)S(1)}, bf16[128,512]{1,0:T(8,128)(2,1)S(1)}, u32[]{:S(2)}, u32[]{:S(2)}) collective-permute-start(bf16[128,512]{1,0:T(8,128)(2,1)S(1)} %add_convert_fusion.6), channel_id=1, source_target_pairs={{0,2},{1,3},{2,0},{3,1},{4,6},{5,7},{6,4},{7,5},{8,10},{9,11},{10,... | collective-permute-start | bytes 393224 | tf_op jit(solution)/shard_map/ppermute | solution.py:295
  77.6 6.3 %collective-permute-start.26 = (bf16[128,512]{1,0:T(8,128)(2,1)S(1)}, bf16[128,512]{1,0:T(8,128)(2,1)S(1)}, u32[]{:S(2)}, u32[]{:S(2)}) collective-permute-start(bf16[128,512]{1,0:T(8,128)(2,1)S(1)} %get-tuple-element.51), channel_id=1, source_target_pairs={{0,1},{1,0},{2,3},{3,2},{4,5},{5,4},{6,7},{7,6},{8,9},{9,8},{10,11... | collective-permute-start | bytes 393224 | tf_op jit(solution)/shard_map/ppermute | solution.py:295
  83.6 1.5 collective-permute-start.12
  84.0 13.1 %collective-permute-start.27 = (bf16[128,512]{1,0:T(8,128)(2,1)S(1)}, bf16[128,512]{1,0:T(8,128)(2,1)S(1)}, u32[]{:S(2)}, u32[]{:S(2)}) collective-permute-start(bf16[128,512]{1,0:T(8,128)(2,1)S(1)} %add_convert_fusion.4), channel_id=1, source_target_pairs={{0,2},{1,3},{2,0},{3,1},{4,6},{5,7},{6,4},{7,5},{8,10},{9,11},{10,... | collective-permute-start | bytes 393224 | tf_op jit(solution)/shard_map/ppermute | solution.py:295
  95.4 15.5 %collective-permute-start.14 = (bf16[32,32,256]{2,1,0:T(8,128)(2,1)}, bf16[32,32,256]{2,1,0:T(8,128)(2,1)S(1)}, u32[]{:S(2)}, u32[]{:S(2)}) collective-permute-start(bf16[32,32,256]{2,1,0:T(8,128)(2,1)} %get-tuple-element.35), channel_id=1, source_target_pairs={{0,16},{4,12},{8,24},{12,4},{16,0},{20,28},{24,8},{28,20},{1,17},{... | collective-permute-start | bytes 1572872 | tf_op jit(solution)/shard_map/ppermute | solution.py:292
  97.1 37.4 %copy-start.10 = (bf16[32,32,256]{2,1,0:T(8,128)(2,1)S(1)}, bf16[32,32,256]{2,1,0:T(8,128)(2,1)}, u32[]{:S(2)}) copy-start(bf16[32,32,256]{2,1,0:T(8,128)(2,1)} %get-tuple-element.32) | copy-start | bytes 1572868
  97.1 1.4 collective-permute-start.28
  108.8 32.1 %copy-start.11 = (bf16[32,32,256]{2,1,0:T(8,128)(2,1)S(1)}, bf16[32,32,256]{2,1,0:T(8,128)(2,1)}, u32[]{:S(2)}) copy-start(bf16[32,32,256]{2,1,0:T(8,128)(2,1)} %get-tuple-element.40) | copy-start | bytes 1572868
  108.8 14.4 %collective-permute-start.30 = (bf16[32,32,256]{2,1,0:T(8,128)(2,1)}, bf16[32,32,256]{2,1,0:T(8,128)(2,1)S(1)}, u32[]{:S(2)}, u32[]{:S(2)}) collective-permute-start(bf16[32,32,256]{2,1,0:T(8,128)(2,1)} %get-tuple-element.43), channel_id=1, source_target_pairs={{0,16},{4,12},{8,24},{12,4},{16,0},{20,28},{24,8},{28,20},{1,17},{... | collective-permute-start | bytes 1572872 | tf_op jit(solution)/shard_map/ppermute | solution.py:292
  109.7 24.9 %collective-permute-start.13 = (bf16[32,32,256]{2,1,0:T(8,128)(2,1)}, bf16[32,32,256]{2,1,0:T(8,128)(2,1)}, u32[]{:S(2)}, u32[]{:S(2)}) collective-permute-start(bf16[32,32,256]{2,1,0:T(8,128)(2,1)} %get-tuple-element.33), channel_id=1, source_target_pairs={{0,16},{4,12},{8,24},{12,4},{16,0},{20,28},{24,8},{28,20},{1,17},{... | collective-permute-start | bytes 1572872 | tf_op jit(solution)/shard_map/ppermute | solution.py:292
  111.1 23.4 %collective-permute-start.15 = (bf16[32,32,256]{2,1,0:T(8,128)(2,1)S(1)}, bf16[32,32,256]{2,1,0:T(8,128)(2,1)}, u32[]{:S(2)}, u32[]{:S(2)}) collective-permute-start(bf16[32,32,256]{2,1,0:T(8,128)(2,1)S(1)} %add_convert_fusion.3), channel_id=1, source_target_pairs={{0,8},{4,20},{8,0},{12,28},{16,24},{20,4},{24,16},{28,12},{1,9},{5... | collective-permute-start | bytes 1572872 | tf_op jit(solution)/shard_map/ppermute | solution.py:292
  112.6 28.3 %collective-permute-start.29 = (bf16[32,32,256]{2,1,0:T(8,128)(2,1)}, bf16[32,32,256]{2,1,0:T(8,128)(2,1)}, u32[]{:S(2)}, u32[]{:S(2)}) collective-permute-start(bf16[32,32,256]{2,1,0:T(8,128)(2,1)} %get-tuple-element.41), channel_id=1, source_target_pairs={{0,16},{4,12},{8,24},{12,4},{16,0},{20,28},{24,8},{28,20},{1,17},{... | collective-permute-start | bytes 1572872 | tf_op jit(solution)/shard_map/ppermute | solution.py:292
  123.2 19.3 %copy-start.1 = (bf16[32,64,128]{2,1,0:T(8,128)(2,1)S(1)}, bf16[32,64,128]{2,1,0:T(8,128)(2,1)}, u32[]{:S(2)}) copy-start(bf16[32,64,128]{2,1,0:T(8,128)(2,1)} %param.9) | copy-start | bytes 1572868
  124.5 16.4 %collective-permute-start.31 = (bf16[32,32,256]{2,1,0:T(8,128)(2,1)S(1)}, bf16[32,32,256]{2,1,0:T(8,128)(2,1)}, u32[]{:S(2)}, u32[]{:S(2)}) collective-permute-start(bf16[32,32,256]{2,1,0:T(8,128)(2,1)S(1)} %add_convert_fusion.1), channel_id=1, source_target_pairs={{0,8},{4,20},{8,0},{12,28},{16,24},{20,4},{24,16},{28,12},{1,9},{5... | collective-permute-start | bytes 1572872 | tf_op jit(solution)/shard_map/ppermute | solution.py:292
  136.2 12.1 %collective-permute-start.16 = (bf16[4,4,32,256]{3,2,1,0:T(8,128)(2,1)S(1)}, bf16[4,4,32,256]{3,2,1,0:T(8,128)(2,1)}, u32[]{:S(2)}, u32[]{:S(2)}) collective-permute-start(bf16[4,4,32,256]{3,2,1,0:T(8,128)(2,1)S(1)} %bitcast.103), channel_id=1, source_target_pairs={{0,4},{4,0},{8,12},{12,8},{16,20},{20,16},{24,28},{28,24},{1,5},{5... | collective-permute-start | bytes 786440 | tf_op jit(solution)/shard_map/ppermute | solution.py:288
  142.5 11.4 %collective-permute-start.32 = (bf16[4,4,32,256]{3,2,1,0:T(8,128)(2,1)S(1)}, bf16[4,4,32,256]{3,2,1,0:T(8,128)(2,1)S(1)}, u32[]{:S(2)}, u32[]{:S(2)}) collective-permute-start(bf16[4,4,32,256]{3,2,1,0:T(8,128)(2,1)S(1)} %bitcast.102), channel_id=1, source_target_pairs={{0,4},{4,0},{8,12},{12,8},{16,20},{20,16},{24,28},{28,24},{1,5},{5... | collective-permute-start | bytes 786440 | tf_op jit(solution)/shard_map/ppermute | solution.py:288
  143.3 8.5 %collective-permute-start.20 = (bf16[2,4,64,128]{3,2,1,0:T(8,128)(2,1)S(1)}, bf16[2,4,64,128]{3,2,1,0:T(8,128)(2,1)S(1)}, u32[]{:S(2)}, u32[]{:S(2)}) collective-permute-start(bf16[2,4,64,128]{3,2,1,0:T(8,128)(2,1)S(1)} %get-tuple-element.62), channel_id=1, source_target_pairs={{0,1},{1,0},{2,3},{3,2},{4,5},{5,4},{6,7},{7,6},{8,9},{9,8},{10,11... | collective-permute-start | bytes 393224 | tf_op jit(solution)/shard_map/ppermute | solution.py:295
  145.9 12.9 %collective-permute-start.21 = (bf16[2,4,64,128]{3,2,1,0:T(8,128)(2,1)S(1)}, bf16[2,4,64,128]{3,2,1,0:T(8,128)(2,1)S(1)}, u32[]{:S(2)}, u32[]{:S(2)}) collective-permute-start(bf16[2,4,64,128]{3,2,1,0:T(8,128)(2,1)S(1)} %get-tuple-element.61), channel_id=1, source_target_pairs={{0,2},{1,3},{2,0},{3,1},{4,6},{5,7},{6,4},{7,5},{8,10},{9,11},{10,... | collective-permute-start | bytes 393224 | tf_op jit(solution)/shard_map/ppermute | solution.py:295
  147.1 11.7 %collective-permute-start.22 = (bf16[2,4,64,128]{3,2,1,0:T(8,128)(2,1)S(1)}, bf16[2,4,64,128]{3,2,1,0:T(8,128)(2,1)S(1)}, u32[]{:S(2)}, u32[]{:S(2)}) collective-permute-start(bf16[2,4,64,128]{3,2,1,0:T(8,128)(2,1)S(1)} %get-tuple-element.60), channel_id=1, source_target_pairs={{0,3},{1,2},{2,1},{3,0},{4,7},{5,6},{6,5},{7,4},{8,11},{9,10},{10,... | collective-permute-start | bytes 393224 | tf_op jit(solution)/shard_map/ppermute | solution.py:295
  150.0 16.9 %collective-permute-start.17 = (bf16[2,4,32,256]{3,2,1,0:T(8,128)(2,1)S(1)}, bf16[2,4,32,256]{3,2,1,0:T(8,128)(2,1)S(1)}, u32[]{:S(2)}, u32[]{:S(2)}) collective-permute-start(bf16[2,4,32,256]{3,2,1,0:T(8,128)(2,1)S(1)} %get-tuple-element.54), channel_id=1, source_target_pairs={{0,1},{1,0},{2,3},{3,2},{4,5},{5,4},{6,7},{7,6},{8,9},{9,8},{10,11... | collective-permute-start | bytes 393224 | tf_op jit(solution)/shard_map/ppermute | solution.py:295
  151.7 23.9 %copy-start.12 = (bf16[2,4,64,128]{3,2,1,0:T(8,128)(2,1)}, bf16[2,4,64,128]{3,2,1,0:T(8,128)(2,1)S(1)}, u32[]{:S(2)}) copy-start(bf16[2,4,64,128]{3,2,1,0:T(8,128)(2,1)S(1)} %collective-permute-done.20.refs_5_) | copy-start | bytes 393220
  151.7 23.9 %collective-permute-start.18 = (bf16[2,4,32,256]{3,2,1,0:T(8,128)(2,1)S(1)}, bf16[2,4,32,256]{3,2,1,0:T(8,128)(2,1)S(1)}, u32[]{:S(2)}, u32[]{:S(2)}) collective-permute-start(bf16[2,4,32,256]{3,2,1,0:T(8,128)(2,1)S(1)} %get-tuple-element.55), channel_id=1, source_target_pairs={{0,2},{1,3},{2,0},{3,1},{4,6},{5,7},{6,4},{7,5},{8,10},{9,11},{10,... | collective-permute-start | bytes 393224 | tf_op jit(solution)/shard_map/ppermute | solution.py:295
  153.9 21.7 %collective-permute-start.19 = (bf16[2,4,32,256]{3,2,1,0:T(8,128)(2,1)S(1)}, bf16[2,4,32,256]{3,2,1,0:T(8,128)(2,1)S(1)}, u32[]{:S(2)}, u32[]{:S(2)}) collective-permute-start(bf16[2,4,32,256]{3,2,1,0:T(8,128)(2,1)S(1)} %get-tuple-element.52), channel_id=1, source_target_pairs={{0,3},{1,2},{2,1},{3,0},{4,7},{5,6},{6,5},{7,4},{8,11},{9,10},{10,... | collective-permute-start | bytes 393224 | tf_op jit(solution)/shard_map/ppermute | solution.py:295
  158.8 16.9 %copy-start.13 = (bf16[2,4,64,128]{3,2,1,0:T(8,128)(2,1)}, bf16[2,4,64,128]{3,2,1,0:T(8,128)(2,1)S(1)}, u32[]{:S(2)}) copy-start(bf16[2,4,64,128]{3,2,1,0:T(8,128)(2,1)S(1)} %collective-permute-done.21.refs_6_) | copy-start | bytes 393220
  158.8 23.7 %collective-permute-start.33 = (bf16[2,4,32,256]{3,2,1,0:T(8,128)(2,1)S(1)}, bf16[2,4,32,256]{3,2,1,0:T(8,128)(2,1)S(1)}, u32[]{:S(2)}, u32[]{:S(2)}) collective-permute-start(bf16[2,4,32,256]{3,2,1,0:T(8,128)(2,1)S(1)} %get-tuple-element.66), channel_id=1, source_target_pairs={{0,1},{1,0},{2,3},{3,2},{4,5},{5,4},{6,7},{7,6},{8,9},{9,8},{10,11... | collective-permute-start | bytes 393224 | tf_op jit(solution)/shard_map/ppermute | solution.py:295
  158.8 26.1 %collective-permute-start.34 = (bf16[2,4,32,256]{3,2,1,0:T(8,128)(2,1)S(1)}, bf16[2,4,32,256]{3,2,1,0:T(8,128)(2,1)S(1)}, u32[]{:S(2)}, u32[]{:S(2)}) collective-permute-start(bf16[2,4,32,256]{3,2,1,0:T(8,128)(2,1)S(1)} %get-tuple-element.67), channel_id=1, source_target_pairs={{0,2},{1,3},{2,0},{3,1},{4,6},{5,7},{6,4},{7,5},{8,10},{9,11},{10,... | collective-permute-start | bytes 393224 | tf_op jit(solution)/shard_map/ppermute | solution.py:295
  166.9 18.1 %collective-permute-start.35 = (bf16[2,4,32,256]{3,2,1,0:T(8,128)(2,1)S(1)}, bf16[2,4,32,256]{3,2,1,0:T(8,128)(2,1)S(1)}, u32[]{:S(2)}, u32[]{:S(2)}) collective-permute-start(bf16[2,4,32,256]{3,2,1,0:T(8,128)(2,1)S(1)} %get-tuple-element.64), channel_id=1, source_target_pairs={{0,3},{1,2},{2,1},{3,0},{4,7},{5,6},{6,5},{7,4},{8,11},{9,10},{10,... | collective-permute-start | bytes 393224 | tf_op jit(solution)/shard_map/ppermute | solution.py:295
  179.2 13.2 %collective-permute-start.23 = (bf16[4,64,128]{2,1,0:T(8,128)(2,1)}, bf16[4,64,128]{2,1,0:T(8,128)(2,1)S(1)}, u32[]{:S(2)}, u32[]{:S(2)}) collective-permute-start(bf16[4,64,128]{2,1,0:T(8,128)(2,1)} %get-tuple-element.37), channel_id=1, source_target_pairs={{0,1},{1,0},{2,3},{3,2},{4,5},{5,4},{6,7},{7,6},{8,9},{9,8},{10,11... | collective-permute-start | bytes 196616 | tf_op jit(solution)/shard_map/ppermute | solution.py:295
  182.5 12.3 %collective-permute-start.24 = (bf16[4,64,128]{2,1,0:T(8,128)(2,1)}, bf16[4,64,128]{2,1,0:T(8,128)(2,1)S(1)}, u32[]{:S(2)}, u32[]{:S(2)}) collective-permute-start(bf16[4,64,128]{2,1,0:T(8,128)(2,1)} %get-tuple-element.38), channel_id=1, source_target_pairs={{0,2},{1,3},{2,0},{3,1},{4,6},{5,7},{6,4},{7,5},{8,10},{9,11},{10,... | collective-permute-start | bytes 196616 | tf_op jit(solution)/shard_map/ppermute | solution.py:295
  182.5 12.3 %collective-permute-start.25 = (bf16[4,64,128]{2,1,0:T(8,128)(2,1)}, bf16[4,64,128]{2,1,0:T(8,128)(2,1)S(1)}, u32[]{:S(2)}, u32[]{:S(2)}) collective-permute-start(bf16[4,64,128]{2,1,0:T(8,128)(2,1)} %get-tuple-element.39), channel_id=1, source_target_pairs={{0,3},{1,2},{2,1},{3,0},{4,7},{5,6},{6,5},{7,4},{8,11},{9,10},{10,... | collective-permute-start | bytes 196616 | tf_op jit(solution)/shard_map/ppermute | solution.py:295
  188.5 6.4 %collective-permute-start.36 = (bf16[4,64,128]{2,1,0:T(8,128)(2,1)}, bf16[4,64,128]{2,1,0:T(8,128)(2,1)S(1)}, u32[]{:S(2)}, u32[]{:S(2)}) collective-permute-start(bf16[4,64,128]{2,1,0:T(8,128)(2,1)} %get-tuple-element.45), channel_id=1, source_target_pairs={{0,1},{1,0},{2,3},{3,2},{4,5},{5,4},{6,7},{7,6},{8,9},{9,8},{10,11... | collective-permute-start | bytes 196616 | tf_op jit(solution)/shard_map/ppermute | solution.py:295
  189.6 6.8 %collective-permute-start.37 = (bf16[4,64,128]{2,1,0:T(8,128)(2,1)}, bf16[4,64,128]{2,1,0:T(8,128)(2,1)S(1)}, u32[]{:S(2)}, u32[]{:S(2)}) collective-permute-start(bf16[4,64,128]{2,1,0:T(8,128)(2,1)} %get-tuple-element.46), channel_id=1, source_target_pairs={{0,2},{1,3},{2,0},{3,1},{4,6},{5,7},{6,4},{7,5},{8,10},{9,11},{10,... | collective-permute-start | bytes 196616 | tf_op jit(solution)/shard_map/ppermute | solution.py:295
  192.4 6.3 %collective-permute-start.38 = (bf16[4,64,128]{2,1,0:T(8,128)(2,1)}, bf16[4,64,128]{2,1,0:T(8,128)(2,1)S(1)}, u32[]{:S(2)}, u32[]{:S(2)}) collective-permute-start(bf16[4,64,128]{2,1,0:T(8,128)(2,1)} %get-tuple-element.47), channel_id=1, source_target_pairs={{0,3},{1,2},{2,1},{3,0},{4,7},{5,6},{6,5},{7,4},{8,11},{9,10},{10,... | collective-permute-start | bytes 196616 | tf_op jit(solution)/shard_map/ppermute | solution.py:295
  (17 other events, 83.2 us)
